TPU v7x, 32 devices: a whole 2x2x4 slice. The times are simulated.
32 devices in a mesh: tm: 8 (over z, x), rows: 4 (over y, core).
Axes of the slice: x: 2, y: 2, z: 4, core: 2. Of those that a mesh axis runs over, the one named last changes fastest.
Arguments:
- observations: float32 [8, 2048], P('tm'), may hold values from -48 to 48
- site_ids: int32 [8, 2048], P('tm'), may hold values from 0 to 4095
- counts: int32 [8], P('tm'), may hold values from 1 to 2048, 12288 in all
- frequencies: float32 [128], replicated, may hold values from -3.140625 to 3.140625
- decay: float32 [128], replicated, may hold values from 0.02 to 0.2
- proc_var: float32 [128], replicated, may hold values from 0.05 to 0.2
Outputs:
- smooth_mean: float32 [8, 256], P('tm', 'rows')
- smooth_cov: float32 [8, 256, 256], P('tm', 'rows')
Inputs may be any that keep to these rules, and one draw needn't show every extreme that they name: Step t observes the sites in its first counts[t] slots; the other slots are ignored.
All inputs are finite; a program needn't handle non-finite values. No bound on the sum of `counts` on one device may be relied on, other than what follows from the above.
Results may differ from a plain program's by a relative error of at most 0.0003.
Values sent between devices are 32-bit elements; how exact they have to be, the bound alone decides.
A program may use at most 128 MiB of HBM per device.

v0:
```python
import functools
import math

import jax
import jax.numpy as jnp
from jax import lax
from jax.experimental import pallas as pl
from jax.experimental.pallas import tpu as pltpu
from jax.sharding import PartitionSpec as P

GRID = 4096
OBS_VAR = 64
TOLERANCE = 3e-5
INNER_TOLERANCE = 4e-6
FINE = 16

exact_mode = lax.Precision.HIGHEST


def exact(left, right):
    return jnp.dot(left, right, precision=exact_mode, preferred_element_type=jnp.float32)


def coarse(left, right):
    return jnp.dot(
        left.astype(jnp.bfloat16), right.astype(jnp.bfloat16), preferred_element_type=jnp.float32
    )


def halves(value):
    high = value.astype(jnp.bfloat16)
    return high, (value - high.astype(jnp.float32)).astype(jnp.bfloat16)


def product(left, right):
    left_high, left_low = left if isinstance(left, tuple) else halves(left)
    right_high, right_low = right if isinstance(right, tuple) else halves(right)
    dot = functools.partial(jnp.dot, preferred_element_type=jnp.float32)
    return dot(left_high, right_high) + (dot(left_high, right_low) + dot(left_low, right_high))


def spread_by(value, picks):
    high, low = halves(value)
    picks = picks.astype(jnp.bfloat16)
    dot = functools.partial(jnp.dot, preferred_element_type=jnp.float32)
    return dot(high, picks) + dot(low, picks)


def picked_by(picks, value):
    high, low = halves(value)
    picks = picks.astype(jnp.bfloat16)
    dot = functools.partial(jnp.dot, preferred_element_type=jnp.float32)
    return dot(picks, high) + dot(picks, low)


def parts(value, unit):
    marked = value * unit
    off = value - marked
    column = jnp.sum(marked, axis=1, keepdims=True)
    row = jnp.sum(marked, axis=0, keepdims=True)
    return value, off, halves(off), column, row


def near(left, right):
    return product(left[2], right[2]) + left[3] * right[0] + left[1] * right[4]


def along(row, right):
    return product(row, right[2]) + row * right[4]


def circle(angle):
    square = angle * angle
    cosine = 1.0 / 40320.0 - square * (1.0 / 3628800.0)
    cosine = 1.0 - square * (0.5 - square * (1.0 / 24.0 - square * (1.0 / 720.0 - square * cosine)))
    sine = 1.0 / 5040.0 - square * (1.0 / 362880.0)
    sine = angle * (1.0 - square * (1.0 / 6.0 - square * (1.0 / 120.0 - square * sine)))
    return cosine, sine


def quarter_turn(quadrant, cosine, sine):
    odd = (quadrant & 1) == 1
    new_cosine = jnp.where(odd, sine, cosine)
    new_sine = jnp.where(odd, cosine, sine)
    new_cosine = jnp.where(((quadrant + 1) & 2) == 2, -new_cosine, new_cosine)
    new_sine = jnp.where((quadrant & 2) == 2, -new_sine, new_sine)
    return new_cosine, new_sine


def share_kernel(
    tm_axis, counts_ref, site_ref, obs_ref, freq_ref, decay_ref, var_ref,
    sums_ref, turn_ref, cols_ref, damp_ref, damp_cols_ref, mine, held, send_sem, recv_sem,
):
    count = lax.axis_size(tm_axis)
    own = lax.axis_index(tm_axis)
    sites = site_ref.shape[1]
    modes = freq_ref.shape[1]
    steps = sums_ref.shape[0]
    barrier = pltpu.get_barrier_semaphore()
    for offset in range(1, count):
        pl.semaphore_signal(
            barrier, inc=1, device_id={tm_axis: lax.rem(own + offset, count)},
            device_id_type=pl.DeviceIdType.MESH,
        )

    groups = 2 * modes // FINE
    total = 2 * groups + groups // 2 + FINE
    last = total - FINE
    spot = lax.broadcasted_iota(jnp.int32, (total, sites), 0)
    exponent = jnp.where(spot < groups, spot * FINE - modes, 2 * modes + 1 - (spot - groups) * FINE)
    exponent = jnp.where(spot >= 2 * groups, (spot - 2 * groups) * FINE + 1, exponent)
    exponent = jnp.where(spot >= last, spot - last, exponent)
    phase = (exponent * site_ref[...]) & (GRID - 1)
    quadrant = (phase + GRID // 8) >> int(math.log2(GRID // 4))
    angle = (phase - quadrant * (GRID // 4)).astype(jnp.float32) * (2.0 * math.pi / GRID)
    cosines, sines = quarter_turn(quadrant, *circle(angle))
    slots = lax.broadcasted_iota(jnp.int32, (1, sites), 1)
    weights = jnp.where(slots < counts_ref[0], 1.0, 0.0)
    scale = jnp.where(spot[:last] < 2 * groups, weights, weights * obs_ref[...])
    left = jnp.concatenate([cosines[:last] * scale, sines[:last] * scale], axis=0)
    right = jnp.concatenate([cosines[last:], sines[last:]], axis=0)
    left_high, left_low = halves(left)
    right_high, right_low = halves(right)
    beside = functools.partial(
        lax.dot_general,
        dimension_numbers=(((1,), (1,)), ((), ())),
        preferred_element_type=jnp.float32,
    )
    sums = beside(left_high, right_high) + (beside(left_high, right_low) + beside(left_low, right_high))
    wide = lax.broadcasted_iota(jnp.int32, (2 * FINE, 2 * modes), 1)
    tall = lax.broadcasted_iota(jnp.int32, (2 * FINE, 2 * modes), 0)
    by_cos = spread_by(sums, jnp.where(tall == (wide & (FINE - 1)), 1.0, 0.0))
    by_sin = spread_by(sums, jnp.where(tall - FINE == (wide & (FINE - 1)), 1.0, 0.0))
    one, two = groups, 2 * groups
    cc, cs, sc, ss = by_cos[:last], by_sin[:last], by_cos[last:], by_sin[last:]
    lane = lax.broadcasted_iota(jnp.int32, (groups, 2 * modes), 1)
    keep = jnp.where(lane // FINE == lax.broadcasted_iota(jnp.int32, (groups, 2 * modes), 0), 1.0, 0.0)

    def flat(value):
        return jnp.sum(value * keep[: value.shape[0]], axis=0, keepdims=True)

    near_cos = flat((cc - ss)[:one])
    near_sin = flat((sc + cs)[:one])
    far_cos = flat((cc + ss)[one:two])
    far_sin = flat((sc - cs)[one:two])
    info = jnp.concatenate([flat((cc - ss)[two:])[:, :modes], flat((sc + cs)[two:])[:, :modes]], axis=1)
    empty = jnp.zeros((3, 2 * modes), jnp.float32)
    mine[...] = jnp.concatenate([near_cos, near_sin, far_cos, far_sin, info, empty], axis=0)

    pl.semaphore_wait(barrier, count - 1)
    copies = []
    for offset in range(1, count):
        copy = pltpu.make_async_remote_copy(
            src_ref=mine,
            dst_ref=held.at[offset],
            send_sem=send_sem.at[offset],
            recv_sem=recv_sem.at[offset],
            device_id={tm_axis: lax.rem(own + offset, count)},
            device_id_type=pl.DeviceIdType.MESH,
        )
        copy.start()
        copies.append(copy)

    frequency = freq_ref[...]
    turns = jnp.where(jnp.abs(frequency) > 0.25 * math.pi, 1, 0) + jnp.where(
        jnp.abs(frequency) > 0.75 * math.pi, 1, 0
    )
    turns = jnp.where(frequency < 0.0, -turns, turns)
    share = turns.astype(jnp.float32)
    reduced = (frequency - share * 1.5703125) - share * (0.5 * math.pi - 1.5703125)
    cosine, sine = quarter_turn(turns + 4, *circle(reduced))
    damping = jnp.exp(-decay_ref[...])
    now_cos = jnp.sqrt(var_ref[...])
    now_sin = jnp.zeros_like(now_cos)
    for step in range(steps):
        block = jnp.concatenate([now_cos, now_sin, jnp.zeros((modes - 2, modes), jnp.float32)], axis=0)
        turn_ref[step] = block[:8]
        cols_ref[step] = block.T[:, :8]
        now_cos, now_sin = now_cos * cosine - now_sin * sine, now_cos * sine + now_sin * cosine
    spread = jnp.broadcast_to(damping, (modes, modes))
    damp_ref[...] = spread[:8]
    damp_cols_ref[...] = spread.T[:, :8]

    sums_ref[own] = mine[...]
    for offset in range(1, count):
        copies[offset - 1].wait()
        sums_ref[lax.rem(own + count - offset, count)] = held[offset]


def invert(sources, targets, low, high, tolerance):
    width = sources[0].shape[-1]
    rows = lax.broadcasted_iota(jnp.int32, (width, width), 0)
    unit = jnp.where(rows == lax.broadcasted_iota(jnp.int32, (width, width), 1), 1.0, 0.0)
    center = (high + low) / (high - low)
    slope = 2.0 / (high - low)
    top = 2.0 * center * center - 1.0
    scaled = []
    bound = 0.0
    for source in sources:
        matrix = source[...]
        marked = matrix * unit
        tall = lax.rsqrt(jnp.sum(marked, axis=1, keepdims=True))
        wide = lax.rsqrt(jnp.sum(marked, axis=0, keepdims=True))
        off = (matrix - marked) * tall * wide
        parted = halves(off)
        square = product(parted, parted)
        bound = jnp.maximum(bound, jnp.max(jnp.sum(jnp.abs(square), axis=0, keepdims=True)))
        scaled.append((tall, wide, off, parted[0], square))
    good = bound < 0.81
    bound = jnp.minimum(bound * 1.001, 0.81)
    start = bound / (2.0 - bound)
    gain = 4.0 / ((2.0 - start * start) * (2.0 - bound))
    for source, target, (tall, wide, off, high_off, square) in zip(sources, targets, scaled):
        residue = (2.0 * square - bound * unit) * (1.0 / (2.0 - bound))
        moved = jnp.dot(high_off, residue.astype(jnp.bfloat16), preferred_element_type=jnp.float32)
        taken = gain * (unit - off + residue - moved) * tall * wide
        other = (4.0 * center * slope / top) * unit - (2.0 * slope * slope / top) * source[...]
        target[...] = jnp.where(good, taken, other)

    def body(radius):
        factor = 2.0 / (2.0 - radius * radius)
        residues = []
        for source, target in zip(sources, targets):
            marked = target[...] * unit
            row = jnp.sum(marked, axis=0, keepdims=True)
            matrix = source[...]
            base = matrix * unit
            off = matrix - base
            column = jnp.sum(base, axis=1, keepdims=True)
            residues.append(
                (unit - column * target[...]) - off * row - product(halves(off), target[...] - marked)
            )
        for target, residue in zip(targets, residues):
            target[...] = factor * (target[...] + coarse(target[...], residue))
        return radius * radius / (2.0 - radius * radius)

    first = jnp.where(good, start * start / (2.0 - start * start), 1.0 / top)
    lax.while_loop(lambda radius: radius > tolerance, body, first)


def solve_kernel(
    tm_axis, rows_axis, sums_ref, turn_ref, turn_cols_ref, damp_ref, damp_cols_ref,
    mean_ref, cov_ref, diag, link, back, info, inverse,
):
    steps = sums_ref.shape[0]
    width = sums_ref.shape[2]
    modes = width // 2
    own = lax.axis_index(tm_axis)
    block_row = lax.axis_index(rows_axis)
    rows = lax.broadcasted_iota(jnp.int32, (width, width), 0)
    cols = lax.broadcasted_iota(jnp.int32, (width, width), 1)
    unit = jnp.where(rows == cols, 1.0, 0.0)
    small_rows = lax.broadcasted_iota(jnp.int32, (modes, modes), 0)
    small_cols = lax.broadcasted_iota(jnp.int32, (modes, modes), 1)
    mirror = jnp.where(small_rows + small_cols == modes - 1, 1.0, 0.0)
    scale = 0.5 / (OBS_VAR * modes)
    info_scale = 1.0 / (OBS_VAR * math.sqrt(modes))
    damp = damp_ref[0:1, :]
    damp_col = damp_cols_ref[:, 0:1]
    wide = damp * damp
    damp_sq = jnp.concatenate([wide, wide], axis=1)

    def shifted(row):
        spread = jnp.broadcast_to(row, (modes, width))
        return pltpu.roll(spread, modes, 1, stride=1, stride_axis=0)[:, :modes]

    most = jnp.zeros((1, width), jnp.float32)
    far_all = spread_by(
        jnp.concatenate(
            [shifted(sums_ref[step, row : row + 1, :]) for step in range(steps) for row in (2, 3)], axis=0
        ),
        mirror,
    )
    for step in range(steps):
        near_cos = shifted(sums_ref[step, 0:1, :])
        near_sin = shifted(sums_ref[step, 1:2, :])
        far_cos = far_all[2 * step * modes : (2 * step + 1) * modes]
        far_sin = far_all[(2 * step + 1) * modes : (2 * step + 2) * modes]
        cosines = turn_ref[step, 0:1, :] * scale
        sines = turn_ref[step, 1:2, :] * scale
        cos_col = turn_cols_ref[step, :, 0:1]
        sin_col = turn_cols_ref[step, :, 1:2]
        up_a, up_b = near_cos + far_cos, far_sin + near_sin
        low_a, low_b = far_sin - near_sin, near_cos - far_cos
        up_left, up_right = up_a * cosines + up_b * sines, up_b * cosines - up_a * sines
        low_left, low_right = low_a * cosines + low_b * sines, low_b * cosines - low_a * sines
        top = jnp.concatenate(
            [cos_col * up_left + sin_col * low_left, cos_col * up_right + sin_col * low_right], axis=1
        )
        bottom = jnp.concatenate(
            [cos_col * low_left - sin_col * up_left, cos_col * low_right - sin_col * up_right], axis=1
        )
        whole = jnp.concatenate([top, bottom], axis=0)
        most = jnp.maximum(most, jnp.sum(jnp.abs(whole), axis=0, keepdims=True))
        edge = 1.0 if step in (0, steps - 1) else 1.0 + damp_sq
        diag[step] = whole + unit * edge
        info_cos, info_sin = sums_ref[step, 4:5, :modes], sums_ref[step, 4:5, modes:]
        turn_cos, turn_sin = turn_ref[step, 0:1, :] * info_scale, turn_ref[step, 1:2, :] * info_scale
        turned = jnp.concatenate(
            [turn_cos * info_cos + turn_sin * info_sin, turn_cos * info_sin - turn_sin * info_cos], axis=1
        )
        info[step] = jnp.broadcast_to(turned, (8, width))
    high = jnp.max(most) * 1.001 + (1.0 + 1.001 * jnp.max(wide))

    def low(power):
        return 0.999 * jnp.min((1.0 - wide) / (1.0 - power))

    def place(position, amount, flipped):
        return jnp.where(flipped, amount - 1 - position, position)

    damp_wide = jnp.concatenate([damp, damp], axis=1)
    damp_tall = jnp.concatenate([damp_col, damp_col], axis=0)
    amount, index, level = steps, own, 0
    power = wide
    diag_at, link_at = 0, 0
    while amount > 1:
        half = amount // 2
        flipped = lax.rem(index, 2) == 1
        links = amount - 1
        out_base = diag_at + amount
        chunk = min(4, half)
        for start in range(0, half, chunk):
            picks = [diag_at + place(2 * k + 1, amount, flipped) for k in range(start, start + chunk)]
            invert(
                [diag.at[pick] for pick in picks],
                [inverse.at[k] for k in range(start, start + chunk)],
                low(power),
                high,
                INNER_TOLERANCE,
            )
        for k in range(half):
            kept = diag_at + place(2 * k, amount, flipped)
            diag[out_base + k] = diag[kept]
            info[out_base + k] = info[kept]
        out_links = link_at + (links if level else 0)
        for k in range(half):
            gone = info[diag_at + place(2 * k + 1, amount, flipped)]
            matrix = parts(inverse[k], unit)
            if level == 0:
                moved = damp_tall * matrix[0] * damp_wide
                passed = along(gone, matrix) * damp_wide
                diag[out_base + k] -= moved
                info[out_base + k] += passed
                if k + 1 < half:
                    diag[out_base + k + 1] -= moved
                    info[out_base + k + 1] += passed
                    link[out_links + k] = moved
                continue
            here = link_at + place(2 * k, links, flipped)
            if level == 1:
                forth = revert = parts(link[here], unit)
            else:
                forth, revert = link[here], back[here]
                forth, revert = (
                    parts(jnp.where(flipped, revert, forth), unit),
                    parts(jnp.where(flipped, forth, revert), unit),
                )
            left = parts(near(matrix, revert), unit)
            diag[out_base + k] -= near(forth, left)
            info[out_base + k] += along(gone, left)
            if k + 1 < half:
                after = link_at + place(2 * k + 1, links, flipped)
                if level == 1:
                    next_forth = next_revert = parts(link[after], unit)
                else:
                    next_forth, next_revert = link[after], back[after]
                    next_forth, next_revert = (
                        parts(jnp.where(flipped, next_revert, next_forth), unit),
                        parts(jnp.where(flipped, next_forth, next_revert), unit),
                    )
                right = parts(near(matrix, next_forth), unit)
                diag[out_base + k + 1] -= near(next_revert, right)
                info[out_base + k + 1] += along(gone, right)
                link[out_links + k] = near(forth, right)
                back[out_links + k] = near(next_revert, left)
        index = place(index, amount, flipped) // 2
        diag_at, link_at = out_base, out_links
        amount, level, power = half, level + 1, power * power

    invert([diag.at[diag_at]], [inverse.at[0]], 0.999 * jnp.min(1.0 - wide), high, TOLERANCE)
    result = inverse[0]
    state = along(info[diag_at], parts(result, unit))[0:1]
    cosines, sines = turn_ref[own, 0:1, :], turn_ref[own, 1:2, :]
    cos_col, sin_col = turn_cols_ref[own, :, 0:1], turn_cols_ref[own, :, 1:2]
    left, right = result[:, :modes], result[:, modes:]
    left, right = left * cosines - right * sines, left * sines + right * cosines
    result = jnp.concatenate([left, right], axis=1)
    upper, lower = result[:modes], result[modes:]
    result = jnp.concatenate(
        [cos_col * upper - sin_col * lower, sin_col * upper + cos_col * lower], axis=0
    )
    first, second = state[:, :modes], state[:, modes:]
    state = jnp.concatenate([first * cosines - second * sines, first * sines + second * cosines], axis=1)
    block = cov_ref.shape[1]
    out_rows = lax.broadcasted_iota(jnp.int32, (block, width), 0) + block_row * block
    out_cols = lax.broadcasted_iota(jnp.int32, (block, width), 1)
    pick = jnp.where(out_cols == out_rows // 2 + lax.rem(out_rows, 2) * modes, 1.0, 0.0)
    spread = jnp.where(rows == cols // 2 + lax.rem(cols, 2) * modes, 1.0, 0.0)
    cov_ref[0] = spread_by(picked_by(pick, result), spread)
    means = lax.dot_general(
        jnp.broadcast_to(state, (8, width)), pick, (((1,), (1,)), ((), ())),
        precision=exact_mode, preferred_element_type=jnp.float32,
    )
    mean_ref[...] = means[0:1]


def local(observations, site_ids, counts, frequencies, decay, proc_var):
    modes = frequencies.shape[0]
    width = 2 * modes
    count = lax.axis_size("tm")
    steps = count * observations.shape[0]
    block = width // lax.axis_size("rows")
    vmem = pl.BlockSpec(memory_space=pltpu.VMEM)
    smem = pl.BlockSpec(memory_space=pltpu.SMEM)
    shared = pl.pallas_call(
        functools.partial(share_kernel, "tm"),
        out_shape=(
            jax.ShapeDtypeStruct((steps, 8, width), jnp.float32),
            jax.ShapeDtypeStruct((steps, 8, modes), jnp.float32),
            jax.ShapeDtypeStruct((steps, modes, 8), jnp.float32),
            jax.ShapeDtypeStruct((8, modes), jnp.float32),
            jax.ShapeDtypeStruct((modes, 8), jnp.float32),
        ),
        in_specs=[smem] + [vmem] * 5,
        out_specs=(vmem,) * 5,
        scratch_shapes=[
            pltpu.VMEM((8, width), jnp.float32),
            pltpu.VMEM((count, 8, width), jnp.float32),
            pltpu.SemaphoreType.DMA((count,)),
            pltpu.SemaphoreType.DMA((count,)),
        ],
        compiler_params=pltpu.CompilerParams(collective_id=0, has_side_effects=True),
        name="share",
    )(counts, site_ids, observations, frequencies[None], decay[None], proc_var[None])
    return pl.pallas_call(
        functools.partial(solve_kernel, "tm", "rows"),
        out_shape=(
            jax.ShapeDtypeStruct((1, block), jnp.float32),
            jax.ShapeDtypeStruct((1, block, width), jnp.float32),
        ),
        in_specs=[vmem] * 5,
        out_specs=(vmem, vmem),
        scratch_shapes=[
            pltpu.VMEM((2 * steps, width, width), jnp.float32),
            pltpu.VMEM((steps, width, width), jnp.float32),
            pltpu.VMEM((steps, width, width), jnp.float32),
            pltpu.VMEM((2 * steps, 8, width), jnp.float32),
            pltpu.VMEM((max(1, steps // 2), width, width), jnp.float32),
        ],
        name="solve",
    )(*shared)


def solution(mesh):
    return jax.shard_map(
        local,
        mesh=mesh,
        in_specs=(P("tm", None), P("tm", None), P("tm"), P(), P(), P()),
        out_specs=(P("tm", "rows"), P("tm", "rows", None)),
        check_vma=False,
    )
```

profile of v0, /device:TPU:0, one launch (start us, length us, event | category | flops | bytes accessed | tf_op | source)
XLA Modules:
  0.0 24.8 jit_solution(11066470817780230976)
XLA Ops:
  1.3 10.7 %share.1 = (f32[8,8,256]{2,1,0:T(8,128)}, f32[8,8,128]{2,1,0:T(8,128)}, f32[8,128,8]{2,1,0:T(8,128)}, f32[8,128]{1,0:T(8,128)}, f32[128,8]{1,0:T(8,128)}) custom-call(s32[1]{0:T(128)S(6)} %copy.8.counts_ref, s32[1,2048]{1,0:T(1,128)} %site_ref.1, f32[1,2048]{1,0:T(1,128)} %obs_ref.1, f32[1,128]{1,0:T(1,128)} %bitcast.3, f32[1,128]{1,0:T(1,128)} %bitcast.4, ...), custom_call_target="tpu_custom_call" | custom-call | tf_op jit(solution)/shard_map/share/pallas_call | solution.py:415
  12.0 12.8 %solve.1 = (f32[1,64]{1,0:T(1,128)}, f32[1,64,256]{2,1,0:T(8,128)}) custom-call(f32[8,8,256]{2,1,0:T(8,128)} %get-tuple-element.7.sums_ref, f32[8,8,128]{2,1,0:T(8,128)} %get-tuple-element.8.turn_ref, f32[8,128,8]{2,1,0:T(8,128)} %get-tuple-element.9.turn_cols_ref, f32[8,128]{1,0:T(8,128)} %get-tuple-element.10.damp_ref, ...), custom_call_target="tpu_custom_call" | custom-call | tf_op jit(solution)/shard_map/solve/pallas_call | solution.py:435
where the time goes:
time: 25 us; the launch traced here: 24.8 us
  Pallas kernels  23.5 us (94%)
  between operations  1.28 us (5%)
    pallas_call x1, Pallas kernels, local(): pl.pallas_call(functools.partial(solve_kernel, 'tm', 'rows'), out_shape=(...  12.8 us
    pallas_call x1, Pallas kernels, local(): pl.pallas_call(functools.partial(share_kernel, 'tm'), out_shape=(jax.Shap...  10.7 us

commit v1 on v0

v1 whole, which is shorter than its diff:
```python
import functools
import math

import jax
import jax.numpy as jnp
from jax import lax
from jax.experimental import pallas as pl
from jax.experimental.pallas import tpu as pltpu
from jax.sharding import PartitionSpec as P

GRID = 4096
OBS_VAR = 64
FINE = 16
TILE = 8
CHAIN_BOUND = 2.5e-3
LAST_BOUND = 5e-3
TOLERANCE = 1e-6

exact_mode = lax.Precision.HIGHEST


def exact(left, right):
    return jnp.dot(left, right, precision=exact_mode, preferred_element_type=jnp.float32)


dot = functools.partial(jnp.dot, preferred_element_type=jnp.float32)


def halves(value):
    high = value.astype(jnp.bfloat16)
    return high, (value - high.astype(jnp.float32)).astype(jnp.bfloat16)


def spread_by(value, picks):
    high, low = halves(value)
    picks = picks.astype(jnp.bfloat16)
    return dot(high, picks) + dot(low, picks)


def circle(angle):
    square = angle * angle
    cosine = 1.0 / 40320.0 - square * (1.0 / 3628800.0)
    cosine = 1.0 - square * (0.5 - square * (1.0 / 24.0 - square * (1.0 / 720.0 - square * cosine)))
    sine = 1.0 / 5040.0 - square * (1.0 / 362880.0)
    sine = angle * (1.0 - square * (1.0 / 6.0 - square * (1.0 / 120.0 - square * sine)))
    return cosine, sine


def quarter_turn(quadrant, cosine, sine):
    odd = (quadrant & 1) == 1
    new_cosine = jnp.where(odd, sine, cosine)
    new_sine = jnp.where(odd, cosine, sine)
    new_cosine = jnp.where(((quadrant + 1) & 2) == 2, -new_cosine, new_cosine)
    new_sine = jnp.where((quadrant & 2) == 2, -new_sine, new_sine)
    return new_cosine, new_sine


def share_kernel(
    tm_axis, counts_ref, site_ref, obs_ref, freq_ref, decay_ref, var_ref,
    sums_ref, turn_ref, damp_ref, mine, held, send_sem, recv_sem,
):
    count = lax.axis_size(tm_axis)
    own = lax.axis_index(tm_axis)
    sites = site_ref.shape[1]
    modes = freq_ref.shape[1]
    steps = sums_ref.shape[0]
    barrier = pltpu.get_barrier_semaphore()
    for offset in range(1, count):
        pl.semaphore_signal(
            barrier, inc=1, device_id={tm_axis: lax.rem(own + offset, count)},
            device_id_type=pl.DeviceIdType.MESH,
        )

    frequency = freq_ref[...]
    turns = jnp.where(jnp.abs(frequency) > 0.25 * math.pi, 1, 0) + jnp.where(
        jnp.abs(frequency) > 0.75 * math.pi, 1, 0
    )
    turns = jnp.where(frequency < 0.0, -turns, turns)
    share = turns.astype(jnp.float32)
    reduced = (frequency - share * 1.5703125) - share * (0.5 * math.pi - 1.5703125)
    cosine, sine = quarter_turn(turns + 4, *circle(reduced))
    now_cos = jnp.sqrt(var_ref[...])
    now_sin = jnp.zeros_like(now_cos)
    own_cos, own_sin = now_cos, now_sin
    for step in range(steps):
        turn_ref[step, 0:1, :] = now_cos
        turn_ref[step, 1:2, :] = now_sin
        own_cos = jnp.where(own == step, now_cos, own_cos)
        own_sin = jnp.where(own == step, now_sin, own_sin)
        now_cos, now_sin = now_cos * cosine - now_sin * sine, now_cos * sine + now_sin * cosine
    damp_ref[...] = jnp.broadcast_to(jnp.exp(-decay_ref[...]), damp_ref.shape)

    groups = 2 * modes // FINE
    total = 2 * groups + groups // 2 + FINE
    last = total - FINE
    spot = lax.broadcasted_iota(jnp.int32, (total, sites), 0)
    exponent = jnp.where(spot < groups, spot * FINE - modes, (spot - groups) * FINE + 2)
    exponent = jnp.where(spot >= 2 * groups, (spot - 2 * groups) * FINE + 1, exponent)
    exponent = jnp.where(spot >= last, spot - last, exponent)
    phase = (exponent * site_ref[...]) & (GRID - 1)
    quadrant = (phase + GRID // 8) >> int(math.log2(GRID // 4))
    angle = (phase - quadrant * (GRID // 4)).astype(jnp.float32) * (2.0 * math.pi / GRID)
    cosines, sines = quarter_turn(quadrant, *circle(angle))
    slots = lax.broadcasted_iota(jnp.int32, (1, sites), 1)
    weights = jnp.where(slots < counts_ref[0], 1.0, 0.0)
    scale = jnp.where(spot[:last] < 2 * groups, weights, weights * obs_ref[...])
    left = jnp.concatenate([cosines[:last] * scale, sines[:last] * scale], axis=0)
    right = jnp.concatenate([cosines[last:], sines[last:]], axis=0)
    left_high, left_low = halves(left)
    right_high, right_low = halves(right)
    beside = functools.partial(
        lax.dot_general,
        dimension_numbers=(((1,), (1,)), ((), ())),
        preferred_element_type=jnp.float32,
    )
    sums = beside(left_high, right_high) + (beside(left_high, right_low) + beside(left_low, right_high))
    width = 3 * modes
    tall = lax.broadcasted_iota(jnp.int32, (2 * FINE, width), 0)
    wide = lax.broadcasted_iota(jnp.int32, (2 * FINE, width), 1)
    wide = jnp.where(wide < 2 * modes, wide, 2 * (wide - 2 * modes))
    by_cos = spread_by(sums, jnp.where(tall == (wide & (FINE - 1)), 1.0, 0.0))
    by_sin = spread_by(sums, jnp.where(tall - FINE == (wide & (FINE - 1)), 1.0, 0.0))
    one, two = groups, 2 * groups
    real = by_cos[:last] - by_sin[last:]
    imaginary = by_cos[last:] + by_sin[:last]
    lane = lax.broadcasted_iota(jnp.int32, (groups, width), 1)
    lane = jnp.where(lane < 2 * modes, lane, 2 * (lane - 2 * modes))
    keep = jnp.where(lane // FINE == lax.broadcasted_iota(jnp.int32, (groups, width), 0), 1.0, 0.0)

    def flat(value):
        return jnp.sum(value * keep[: value.shape[0]], axis=0, keepdims=True)

    near_cos, near_sin = flat(real[:one])[:, : 2 * modes], flat(imaginary[:one])[:, : 2 * modes]
    far_cos, far_sin = flat(real[one:two]), flat(imaginary[one:two])
    info_cos, info_sin = flat(real[two:])[:, :modes], flat(imaginary[two:])[:, :modes]
    info_scale = 1.0 / (OBS_VAR * math.sqrt(modes))
    turn_cos, turn_sin = own_cos * info_scale, own_sin * info_scale
    info = jnp.concatenate(
        [turn_cos * info_cos + turn_sin * info_sin, turn_cos * info_sin - turn_sin * info_cos], axis=1
    )
    square, cross = own_cos * own_cos, own_sin * own_sin
    level = (square + cross) * near_cos[:, modes : modes + 1]
    swing = (square - cross) * far_cos[:, 2 * modes :] + (2.0 * own_cos * own_sin) * far_sin[:, 2 * modes :]
    weight = jnp.concatenate([level + swing, level - swing], axis=1) * (0.5 / (OBS_VAR * modes))
    empty = jnp.zeros((2, 2 * modes), jnp.float32)
    mine[...] = jnp.concatenate(
        [near_cos, near_sin, far_cos[:, : 2 * modes], far_sin[:, : 2 * modes], info, weight, empty], axis=0
    )

    pl.semaphore_wait(barrier, count - 1)
    copies = []
    for offset in range(1, count):
        copy = pltpu.make_async_remote_copy(
            src_ref=mine,
            dst_ref=held.at[offset],
            send_sem=send_sem.at[offset],
            recv_sem=recv_sem.at[offset],
            device_id={tm_axis: lax.rem(own + offset, count)},
            device_id_type=pl.DeviceIdType.MESH,
        )
        copy.start()
        copies.append(copy)
    sums_ref[own] = mine[...]
    for offset in range(1, count):
        copies[offset - 1].wait()
        sums_ref[lax.rem(own + count - offset, count)] = held[offset]


def solve_kernel(
    tm_axis, rows_axis, sums_ref, turn_ref, damp_ref, mean_ref, cov_ref,
    tab, cols, gain, told, fresh, main, full, kept, narrow, squared, lhs, rhs, answer, spare, result,
):
    steps = sums_ref.shape[0]
    width = sums_ref.shape[2]
    modes = width // 2
    block = cov_ref.shape[1]
    own = lax.axis_index(tm_axis)
    block_row = lax.axis_index(rows_axis)
    links = steps - 1
    sides = (slice(0, modes), slice(modes, width))
    root = math.sqrt(0.5 / (OBS_VAR * modes))
    damp = damp_ref[0:1, :]
    damp_sq = damp * damp
    lane = lax.broadcasted_iota(jnp.int32, (TILE, modes), 1)
    sub = lax.broadcasted_iota(jnp.int32, (TILE, modes), 0)

    def node(i):
        return own if i == links else jnp.where(own > i, i, links - (i - own))

    def inverse_root(value):
        guess = lax.rsqrt(value)
        return guess * (1.5 - 0.5 * value * guess * guess)

    def load(ref, index, row):
        return tuple(ref[index, row : row + 1, side] for side in sides)

    def put(i, scaled, joins):
        cosines, sines = turn_ref[node(i), 0:1, :] * root, turn_ref[node(i), 1:2, :] * root
        rows = (cosines * scaled[0], sines * scaled[0], cosines * scaled[1], sines * scaled[1], *joins)
        for k, row in enumerate(rows):
            tab[TILE * i + k : TILE * i + k + 1, :] = row

    scaled = None
    for i in range(links):
        at = node(i)
        inner = jnp.where(jnp.logical_or(at == 0, at == links), 0.0, 1.0)
        keep = jnp.where(own == i, 0.0, 1.0) if i else 0.0
        level = [1.0 + inner * damp_sq + weight for weight in load(sums_ref, at, 5)]
        if i:
            level = [value - (keep * damp_sq) * (old * old) for value, old in zip(level, scaled)]
        new = [inverse_root(value) for value in level]
        joins = [(keep * damp) * value * old for value, old in zip(new, scaled)] if i else [jnp.zeros_like(damp)] * 2
        put(i, new, joins)
        for side, value, told_info in zip(sides, new, load(sums_ref, at, 4)):
            gain[i, 0:1, side] = value
            told[i, 0:1, side] = value * told_info
        scaled = new
    before = jnp.maximum(own - 1, 0)
    has_left, has_right = jnp.where(own > 0, 1.0, 0.0), jnp.where(own < links, 1.0, 0.0)
    left, right = load(gain, before, 0), scaled
    level = [
        1.0 + (has_left * has_right) * damp_sq + weight
        - (has_left * damp_sq) * (a * a) - (has_right * damp_sq) * (b * b)
        for weight, a, b in zip(load(sums_ref, own, 5), left, right)
    ]
    new = [inverse_root(value) for value in level]
    put(
        links, new,
        [(has_left * damp) * value * old for value, old in zip(new, left)]
        + [(has_right * damp) * value * old for value, old in zip(new, right)],
    )
    for side, value, told_info in zip(sides, new, load(sums_ref, own, 4)):
        gain[links, 0:1, side] = value
        told[links, 0:1, side] = value * told_info
    for chunk in range(tab.shape[0] // modes):
        cols[chunk] = tab[chunk * modes : (chunk + 1) * modes, :].T

    def row_of(i, k):
        return tab[TILE * i + k : TILE * i + k + 1, :]

    def col_of(i, k, rows):
        at = TILE * i + k
        return jnp.broadcast_to(cols[at // modes, rows, at % modes : at % modes + 1], (rows.stop - rows.start, modes))

    def build(i):
        at = node(i)
        bases = []
        for row in range(4):
            base = jnp.broadcast_to(sums_ref[at, row : row + 1, :], (TILE, width))
            if row < 2:
                base = pltpu.roll(base, 0, 1, stride=1, stride_axis=0)
                bases.append((base[:, :modes], base[:, modes:]))
            else:
                base = pltpu.roll(base, width - TILE + 1, 1, stride=1, stride_axis=0)
                bases.append([jnp.take_along_axis(base[:, side], TILE - 1 - sub, axis=0) for side in sides])
        cos_l, sin_l, cos_r, sin_r = [jnp.broadcast_to(row_of(i, k), (TILE, modes)) for k in range(4)]
        for q in range(modes // TILE):
            shift = TILE * q
            rows = slice(shift, shift + TILE)

            def moved(low, high, edge, amount):
                value = jnp.where(lane >= edge, low, high) if edge else low
                return pltpu.roll(value, amount, 1) if amount % modes else value

            near_cos, near_sin = [
                moved(low, high, modes - shift, shift) if shift else high for low, high in bases[:2]
            ]
            far_cos, far_sin = [moved(low, high, shift, modes - shift) for low, high in bases[2:]]
            up_a, up_b = near_cos + far_cos, far_sin + near_sin
            low_a, low_b = far_sin - near_sin, near_cos - far_cos
            up_left, up_right = up_a * cos_l + up_b * sin_l, up_b * cos_r - up_a * sin_r
            low_left, low_right = low_a * cos_l + low_b * sin_l, low_b * cos_r - low_a * sin_r
            cos_t, sin_t, cos_b, sin_b = [col_of(i, k, rows) for k in range(4)]
            off = lane != sub + shift
            under = slice(modes + shift, modes + shift + TILE)
            fresh[i, rows, sides[0]] = jnp.where(off, cos_t * up_left + sin_t * low_left, 0.0)
            fresh[i, rows, sides[1]] = cos_t * up_right + sin_t * low_right
            fresh[i, under, sides[0]] = cos_b * low_left - sin_b * up_left
            fresh[i, under, sides[1]] = jnp.where(off, cos_b * low_right - sin_b * up_right, 0.0)

    pair = 2 * TILE
    strips = [
        (half, slice(start, start + pair), slice(half * modes + start, half * modes + start + pair))
        for half in range(2) for start in range(0, modes, pair)
    ]
    pair_lane = lax.broadcasted_iota(jnp.int32, (pair, modes), 1)
    pair_sub = lax.broadcasted_iota(jnp.int32, (pair, modes), 0)

    def flow(i, state, third):
        sums = [jnp.zeros((pair, modes), jnp.float32) for _ in sides]
        for half, part, rows in strips:
            parts = []
            for k, side in enumerate(sides):
                value = main[i, rows, side] + third[rows, side]
                full[i, rows, side] = value
                parts.append(value * state[k])
            column = jnp.sum(parts[0] + parts[1], axis=1, keepdims=True)
            sums[half] += jnp.where(pair_lane == pair_sub + part.start, column, 0.0)
        moved = [value - jnp.sum(total, axis=0, keepdims=True) for value, total in zip(state, sums)]
        for side, value in zip(sides, moved):
            gain[i, 1:2, side] = value
        return moved

    build(0)
    third, state, most = None, None, jnp.zeros((TILE, width), jnp.float32)
    for i in range(links):
        slot = i % 2
        for half, part, rows in strips:
            join = col_of(i, 4 + half, part) if i else None
            for k, side in enumerate(sides):
                value = fresh[i, rows, side]
                if i:
                    value = value + join * (main[i - 1, rows, side] * row_of(i, 4 + k))
                    kept[slot, rows, side] = value
                narrow[slot, rows, side] = value.astype(jnp.bfloat16)
        square = dot(narrow[slot], narrow[slot])
        build(i + 1)
        if i:
            moved = flow(i - 1, state, third)
        state = [told[i, 0:1, side] + (row_of(i, 4 + k) * moved[k] if i else 0.0) for k, side in enumerate(sides)]
        for half, part, rows in strips:
            join = col_of(i, 4 + half, part) if i else None
            for k, side in enumerate(sides):
                value = square[rows, side]
                squared[slot, rows, side] = value.astype(jnp.bfloat16)
                if i:
                    main[i, rows, side] = (kept[slot, rows, side] - value) + join * (third[rows, side] * row_of(i, 4 + k))
                else:
                    main[i, rows, side] = fresh[i, rows, side] - value
        weight = jnp.abs(square)
        total = weight[:TILE]
        for start in range(TILE, width, TILE):
            total = total + weight[start : start + TILE]
        most = jnp.maximum(most, jnp.broadcast_to(jnp.sum(total, axis=0, keepdims=True), most.shape))
        third = dot(squared[slot], narrow[slot])
    moved = flow(links - 1, state, third)

    odd = lhs.shape[0] - width
    height = block + pair
    tall = lax.broadcasted_iota(jnp.int32, (block, modes), 0)
    wide = lax.broadcasted_iota(jnp.int32, (block, modes), 1)
    hit = wide == (tall + block_row * block) // 2
    even = tall % 2 == 0
    cos_l, sin_l, cos_r, sin_r = [row_of(links, k) * (1.0 / root) for k in range(4)]

    def last_state():
        joins = [row_of(links, k) for k in range(4, 8)]
        return [
            told[links, 0:1, side] + joins[k] * gain[before, 1:2, side] + joins[2 + k] * gain[links - 1, 1:2, side]
            for k, side in enumerate(sides)
        ]

    def pose(state):
        spare[:block, sides[0]] = jnp.where(hit, jnp.where(even, cos_l, sin_l), 0.0)
        spare[:block, sides[1]] = jnp.where(hit, jnp.where(even, -sin_r, cos_r), 0.0)
        for side, value in zip(sides, state):
            spare[block:, side] = jnp.where(pair_sub == 0, value, 0.0)

    def split(value, rows, side):
        high, low = halves(value)
        at, deep = side.start, width
        lhs[rows, at : at + modes] = high
        lhs[rows, deep + at : deep + at + modes] = high
        lhs[rows, 2 * deep + at : 2 * deep + at + modes] = low
        return high, low

    for half, part, rows in strips:
        first, second = col_of(links, 4 + half, part), col_of(links, 6 + half, part)
        for k, side in enumerate(sides):
            value = fresh[links, rows, side] + first * (full[before, rows, side] * row_of(links, 4 + k))
            value = value + second * (full[links - 1, rows, side] * row_of(links, 6 + k))
            high, low = split(value, rows, side)
            for number, piece in enumerate((high, low, high)):
                rhs[0, number * width + rows.start : number * width + rows.stop, side] = piece
    pose(last_state())
    asked = slice(width, width + height)
    for side in sides:
        split(spare[:, side], asked, side)
    both = dot(lhs[...], rhs[0])
    square = both[:width]
    first = spare[...] - both[width:]
    for side in sides:
        split(first[:, side], asked, side)
    for half, part, rows in strips:
        for side in sides:
            high, low = halves(square[rows, side])
            for number, piece in enumerate((high, low, high)):
                rhs[1, number * width + rows.start : number * width + rows.stop, side] = piece
    second = first + dot(lhs[asked, :], rhs[1])
    fourth = dot(rhs[1, :width, :], rhs[1, :width, :])
    weight = jnp.abs(fourth)
    total = weight[:TILE]
    for start in range(TILE, width, TILE):
        total = total + weight[start : start + TILE]
    total = jnp.sum(total, axis=0, keepdims=True)
    answer[...] = second + dot(second.astype(jnp.bfloat16), fourth.astype(jnp.bfloat16))
    good = jnp.logical_and(jnp.max(most) <= CHAIN_BOUND, jnp.max(total) <= LAST_BOUND)

    @pl.when(jnp.logical_not(good))
    def _():
        rows = lax.broadcasted_iota(jnp.int32, (width, width), 0)
        unit = rows == lax.broadcasted_iota(jnp.int32, (width, width), 1)
        source, target = result.at[0], result.at[1]

        def both_ways(value, i, k):
            row = jnp.concatenate([tab[pl.ds(TILE * i + k, 1), :], tab[pl.ds(TILE * i + k + 1, 1), :]], axis=1)
            column = jnp.sum(jnp.where(unit, row, 0.0), axis=1, keepdims=True)
            return column * value * row

        def invert(low):
            high = 1.001 * jnp.max(jnp.sum(jnp.abs(source[...]), axis=0, keepdims=True))
            low = jnp.minimum(low, 0.5 * high)
            center = (high + low) / (high - low)
            slope = 2.0 / (high - low)
            top = 2.0 * center * center - 1.0
            target[...] = jnp.where(unit, 4.0 * center * slope / top, 0.0) - (2.0 * slope * slope / top) * source[...]

            def improve(radius):
                factor = 2.0 / (2.0 - radius * radius)
                residue = jnp.where(unit, 1.0, 0.0) - exact(source[...], target[...])
                target[...] = factor * (target[...] + exact(target[...], residue))
                return radius * radius / (2.0 - radius * radius)

            lax.while_loop(lambda radius: radius > TOLERANCE, improve, 1.0 / top)

        full[0] = jnp.zeros((width, width), jnp.float32)
        gain[0, 1:2, :] = jnp.zeros((1, width), jnp.float32)

        def advance(i, carry):
            old = jnp.maximum(i - 1, 0)
            source[...] = jnp.where(unit, 1.0, 0.0) + fresh[i] + both_ways(full[old], i, 4)
            scaling = gain[i, 0:1, :]
            invert(0.999 * jnp.min(scaling * scaling))
            join = jnp.concatenate([tab[pl.ds(TILE * i + 4, 1), :], tab[pl.ds(TILE * i + 5, 1), :]], axis=1)
            state = told[i, 0:1, :] + join * gain[old, 1:2, :]
            gain[i, 1:2, :] = exact(jnp.broadcast_to(state, (TILE, width)), target[...])[0:1]
            full[i] = jnp.where(unit, 1.0, 0.0) - target[...]
            return carry

        lax.fori_loop(0, links, advance, 0)
        source[...] = (
            jnp.where(unit, 1.0, 0.0) + fresh[links]
            + both_ways(full[before], links, 4) + both_ways(full[links - 1], links, 6)
        )
        scaling = gain[links, 0:1, :]
        invert(0.999 * jnp.min(1.0 - damp_sq) * jnp.min(scaling * scaling))
        pose(last_state())
        answer[...] = exact(spare[...], target[...])

    left, right = answer[:, sides[0]], answer[:, sides[1]]
    left, right = left * cos_l - right * sin_r, left * sin_l + right * cos_r
    wide = lax.broadcasted_iota(jnp.int32, (height, modes), 1)
    out = []
    for number in range(2):
        pick = wide // 2 + number * (modes // 2)
        out.append(
            jnp.where(wide % 2 == 0, jnp.take_along_axis(left, pick, axis=1), jnp.take_along_axis(right, pick, axis=1))
        )
    for side, value in zip(sides, out):
        cov_ref[0, :, side] = value[:block]
    means = jnp.concatenate([value[block : block + TILE] for value in out], axis=1)
    mean_ref[...] = pltpu.roll(means, width - block_row * block, 1)[0:1, :block]


def local(observations, site_ids, counts, frequencies, decay, proc_var):
    modes = frequencies.shape[0]
    width = 2 * modes
    count = lax.axis_size("tm")
    steps = count * observations.shape[0]
    block = width // lax.axis_size("rows")
    height = block + 2 * TILE
    table = -(-TILE * steps // modes) * modes
    vmem = pl.BlockSpec(memory_space=pltpu.VMEM)
    smem = pl.BlockSpec(memory_space=pltpu.SMEM)
    shared = pl.pallas_call(
        functools.partial(share_kernel, "tm"),
        out_shape=(
            jax.ShapeDtypeStruct((steps, 8, width), jnp.float32),
            jax.ShapeDtypeStruct((steps, 8, modes), jnp.float32),
            jax.ShapeDtypeStruct((8, modes), jnp.float32),
        ),
        in_specs=[smem] + [vmem] * 5,
        out_specs=(vmem,) * 3,
        scratch_shapes=[
            pltpu.VMEM((8, width), jnp.float32),
            pltpu.VMEM((count, 8, width), jnp.float32),
            pltpu.SemaphoreType.DMA((count,)),
            pltpu.SemaphoreType.DMA((count,)),
        ],
        compiler_params=pltpu.CompilerParams(collective_id=0, has_side_effects=True, vmem_limit_bytes=16 << 20),
        name="share",
    )(counts, site_ids, observations, frequencies[None], decay[None], proc_var[None])
    return pl.pallas_call(
        functools.partial(solve_kernel, "tm", "rows"),
        out_shape=(
            jax.ShapeDtypeStruct((1, block), jnp.float32),
            jax.ShapeDtypeStruct((1, block, width), jnp.float32),
        ),
        in_specs=[vmem] * 3,
        out_specs=(vmem, vmem),
        scratch_shapes=[
            pltpu.VMEM((table, modes), jnp.float32),
            pltpu.VMEM((table // modes, modes, modes), jnp.float32),
            pltpu.VMEM((steps, 8, width), jnp.float32),
            pltpu.VMEM((steps, 8, width), jnp.float32),
            pltpu.VMEM((steps, width, width), jnp.float32),
            pltpu.VMEM((steps - 1, width, width), jnp.float32),
            pltpu.VMEM((steps - 1, width, width), jnp.float32),
            pltpu.VMEM((2, width, width), jnp.float32),
            pltpu.VMEM((2, width, width), jnp.bfloat16),
            pltpu.VMEM((2, width, width), jnp.bfloat16),
            pltpu.VMEM((width + height, 3 * width), jnp.bfloat16),
            pltpu.VMEM((2, 3 * width, width), jnp.bfloat16),
            pltpu.VMEM((height, width), jnp.float32),
            pltpu.VMEM((height, width), jnp.float32),
            pltpu.VMEM((2, width, width), jnp.float32),
        ],
        compiler_params=pltpu.CompilerParams(vmem_limit_bytes=40 << 20),
        name="solve",
    )(*shared)


def solution(mesh):
    return jax.shard_map(
        local,
        mesh=mesh,
        in_specs=(P("tm", None), P("tm", None), P("tm"), P(), P(), P()),
        out_specs=(P("tm", "rows"), P("tm", "rows", None)),
        check_vma=False,
    )
```

time: 25 us -> 18.3 us (0.73)
  Pallas kernels: 23.5 us -> 14.6 us
  local copies, waits for them, and re-layouts: 0 us -> 2.06 us
    pallas_call x1, Pallas kernels: 12.8 us -> 5.42 us  [local(): pl.pallas_call(functools.partial(solve_kernel, 'tm', 'rows'), out_shape=(...]
    unnamed x0 -> x10, local copies, waits for them, and re-layouts: none -> 2.06 us
    pallas_call x1, Pallas kernels: 10.7 us -> 9.21 us  [local(): pl.pallas_call(functools.partial(share_kernel, 'tm'), out_shape=(jax.Shap...]
where the time goes in v1:
time: 18.3 us; the launch traced here: 18 us
  Pallas kernels  14.6 us (80%)
  local copies, waits for them, and re-layouts  2.06 us (11%)
  between operations  1.31 us (7%)
    pallas_call x1, Pallas kernels, local(): pl.pallas_call(functools.partial(share_kernel, 'tm'), out_shape=(jax.Shap...  9.21 us
    pallas_call x1, Pallas kernels, local(): pl.pallas_call(functools.partial(solve_kernel, 'tm', 'rows'), out_shape=(...  5.42 us
    unnamed x10, local copies, waits for them, and re-layouts  2.06 us

profile of v1, /device:TPU:0, one launch (start us, length us, event | category | flops | bytes accessed | tf_op | source)
XLA Modules:
  0.0 18.0 jit_solution(11223304796368939468)
XLA Ops:
  1.3 0.0 copy-start.2
  1.3 0.0 copy-start.3
  1.3 0.0 copy-start.4
  1.3 0.6 %copy-done.2 = f32[128]{0:T(128)S(1)} copy-done((f32[128]{0:T(128)S(1)}, f32[128]{0:T(128)}, u32[]{:S(2)}) %copy-start.2) | copy-done | bytes 536
  1.9 0.0 copy-done.3
  1.9 0.0 copy-done.4
  2.0 0.0 copy-start
  2.0 0.7 %copy-done = s32[1,2048]{1,0:T(1,128)S(1)} copy-done((s32[1,2048]{1,0:T(1,128)S(1)}, s32[1,2048]{1,0:T(1,128)}, u32[]{:S(2)}) %copy-start) | copy-done | bytes 8216
  2.7 0.0 copy-start.1
  2.7 0.7 %copy-done.1 = f32[1,2048]{1,0:T(1,128)S(1)} copy-done((f32[1,2048]{1,0:T(1,128)S(1)}, f32[1,2048]{1,0:T(1,128)}, u32[]{:S(2)}) %copy-start.1) | copy-done | bytes 8216
  3.4 9.2 %share.1 = (f32[8,8,256]{2,1,0:T(8,128)S(1)}, f32[8,8,128]{2,1,0:T(8,128)S(1)}, f32[8,128]{1,0:T(8,128)S(1)}) custom-call(s32[1]{0:T(128)S(6)} %copy.8.counts_ref, s32[1,2048]{1,0:T(1,128)S(1)} %copy-done, f32[1,2048]{1,0:T(1,128)S(1)} %copy-done.1, f32[1,128]{1,0:T(1,128)S(1)} %bitcast.3, f32[1,128]{1,0:T(1,128)S(1)} %bitcast.4, f32[1,128]{1,0:T(1,128)S(1)} %bitcast.5), custom_call_target="tpu_custom_call" | custom-call | tf_op jit(solution)/shard_map/share/pallas_call | solution.py:475
  12.6 5.4 %solve.1 = (f32[1,64]{1,0:T(1,128)}, f32[1,64,256]{2,1,0:T(8,128)}) custom-call(f32[8,8,256]{2,1,0:T(8,128)S(1)} %get-tuple-element.5.sums_ref, f32[8,8,128]{2,1,0:T(8,128)S(1)} %get-tuple-element.6.turn_ref, f32[8,128]{1,0:T(8,128)S(1)} %get-tuple-element.7.damp_ref), custom_call_target="tpu_custom_call" | custom-call | tf_op jit(solution)/shard_map/solve/pallas_call | solution.py:493
Async XLA Ops:
  1.3 0.7 %copy-start.2 = (f32[128]{0:T(128)S(1)}, f32[128]{0:T(128)}, u32[]{:S(2)}) copy-start(f32[128]{0:T(128)} %param.9) | copy-start | bytes 1540
  1.3 0.7 %copy-start.3 = (f32[128]{0:T(128)S(1)}, f32[128]{0:T(128)}, u32[]{:S(2)}) copy-start(f32[128]{0:T(128)} %param.10) | copy-start | bytes 1540
  1.3 0.7 %copy-start.4 = (f32[128]{0:T(128)S(1)}, f32[128]{0:T(128)}, u32[]{:S(2)}) copy-start(f32[128]{0:T(128)} %param.11) | copy-start | bytes 1540
  2.0 0.7 %copy-start = (s32[1,2048]{1,0:T(1,128)S(1)}, s32[1,2048]{1,0:T(1,128)}, u32[]{:S(2)}) copy-start(s32[1,2048]{1,0:T(1,128)} %site_ref.1) | copy-start | bytes 24580
  2.7 0.7 %copy-start.1 = (f32[1,2048]{1,0:T(1,128)S(1)}, f32[1,2048]{1,0:T(1,128)}, u32[]{:S(2)}) copy-start(f32[1,2048]{1,0:T(1,128)} %obs_ref.1) | copy-start | bytes 24580

commit v2 on v1

v2 whole, which is shorter than its diff:
```python
import functools
import math

import jax
import jax.numpy as jnp
from jax import lax
from jax.experimental import pallas as pl
from jax.experimental.pallas import tpu as pltpu
from jax.sharding import PartitionSpec as P

GRID = 4096
OBS_VAR = 64
FINE = 16
TILE = 8
CHAIN_BOUND = 2.5e-3
LAST_BOUND = 5e-3
TOLERANCE = 1e-6

exact_mode = lax.Precision.HIGHEST


def exact(left, right):
    return jnp.dot(left, right, precision=exact_mode, preferred_element_type=jnp.float32)


dot = functools.partial(jnp.dot, preferred_element_type=jnp.float32)


def halves(value):
    high = value.astype(jnp.bfloat16)
    return high, (value - high.astype(jnp.float32)).astype(jnp.bfloat16)


def spread_by(value, picks):
    high, low = halves(value)
    picks = picks.astype(jnp.bfloat16)
    return dot(high, picks) + dot(low, picks)


def circle(angle):
    square = angle * angle
    cosine = 1.0 / 40320.0 - square * (1.0 / 3628800.0)
    cosine = 1.0 - square * (0.5 - square * (1.0 / 24.0 - square * (1.0 / 720.0 - square * cosine)))
    sine = 1.0 / 5040.0 - square * (1.0 / 362880.0)
    sine = angle * (1.0 - square * (1.0 / 6.0 - square * (1.0 / 120.0 - square * sine)))
    return cosine, sine


def quarter_turn(quadrant, cosine, sine):
    odd = (quadrant & 1) == 1
    new_cosine = jnp.where(odd, sine, cosine)
    new_sine = jnp.where(odd, cosine, sine)
    new_cosine = jnp.where(((quadrant + 1) & 2) == 2, -new_cosine, new_cosine)
    new_sine = jnp.where((quadrant & 2) == 2, -new_sine, new_sine)
    return new_cosine, new_sine


def share_kernel(
    tm_axis, counts_ref, site_hbm, obs_hbm, freq_hbm, decay_hbm, var_hbm,
    sums_ref, turn_ref, tile_ref, damp_ref, site_ref, obs_ref, freq_ref, decay_ref, var_ref,
    mine, held, load_sem, send_sem, recv_sem,
):
    count = lax.axis_size(tm_axis)
    own = lax.axis_index(tm_axis)
    sites = site_ref.shape[1]
    modes = freq_ref.shape[1]
    steps = sums_ref.shape[0]
    barrier = pltpu.get_barrier_semaphore()
    for offset in range(1, count):
        pl.semaphore_signal(
            barrier, inc=1, device_id={tm_axis: lax.rem(own + offset, count)},
            device_id_type=pl.DeviceIdType.MESH,
        )
    loads = [
        pltpu.make_async_copy(source, target, load_sem.at[number])
        for number, (source, target) in enumerate((
            (site_hbm, site_ref), (freq_hbm, freq_ref), (obs_hbm, obs_ref),
            (decay_hbm, decay_ref), (var_hbm, var_ref),
        ))
    ]
    for load in loads:
        load.start()
    for load in loads:
        load.wait()

    frequency = freq_ref[...]
    turns = jnp.where(jnp.abs(frequency) > 0.25 * math.pi, 1, 0) + jnp.where(
        jnp.abs(frequency) > 0.75 * math.pi, 1, 0
    )
    turns = jnp.where(frequency < 0.0, -turns, turns)
    share = turns.astype(jnp.float32)
    reduced = (frequency - share * 1.5703125) - share * (0.5 * math.pi - 1.5703125)
    cosine, sine = quarter_turn(turns + 4, *circle(reduced))
    now_cos = jnp.sqrt(var_ref[...])
    now_sin = jnp.zeros_like(now_cos)
    own_cos, own_sin = now_cos, now_sin
    root = math.sqrt(0.5 / (OBS_VAR * modes))
    for step in range(steps):
        for number, value in enumerate((now_cos * root, now_sin * root, now_cos, now_sin)):
            turn_ref[step, number : number + 1, :] = value
        own_cos = jnp.where(own == step, now_cos, own_cos)
        own_sin = jnp.where(own == step, now_sin, own_sin)
        now_cos, now_sin = now_cos * cosine - now_sin * sine, now_cos * sine + now_sin * cosine
    damp_ref[...] = jnp.broadcast_to(jnp.exp(-decay_ref[...]), damp_ref.shape)

    groups = 2 * modes // FINE
    total = 2 * groups + groups // 2 + FINE
    last = total - FINE
    spot = lax.broadcasted_iota(jnp.int32, (total, sites), 0)
    exponent = jnp.where(spot < groups, spot * FINE - modes, (spot - groups) * FINE + 2)
    exponent = jnp.where(spot >= 2 * groups, (spot - 2 * groups) * FINE + 1, exponent)
    exponent = jnp.where(spot >= last, spot - last, exponent)
    phase = (exponent * site_ref[...]) & (GRID - 1)
    quadrant = (phase + GRID // 8) >> int(math.log2(GRID // 4))
    angle = (phase - quadrant * (GRID // 4)).astype(jnp.float32) * (2.0 * math.pi / GRID)
    cosines, sines = quarter_turn(quadrant, *circle(angle))
    slots = lax.broadcasted_iota(jnp.int32, (1, sites), 1)
    weights = jnp.where(slots < counts_ref[0], 1.0, 0.0)
    scale = jnp.where(spot[:last] < 2 * groups, weights, weights * obs_ref[...])
    left = jnp.concatenate([cosines[:last] * scale, sines[:last] * scale], axis=0)
    right = jnp.concatenate([cosines[last:], sines[last:]], axis=0)
    left_high, left_low = halves(left)
    right_high, right_low = halves(right)
    beside = functools.partial(
        lax.dot_general,
        dimension_numbers=(((1,), (1,)), ((), ())),
        preferred_element_type=jnp.float32,
    )
    sums = beside(left_high, right_high) + (beside(left_high, right_low) + beside(left_low, right_high))
    width = 3 * modes
    tall = lax.broadcasted_iota(jnp.int32, (2 * FINE, width), 0)
    wide = lax.broadcasted_iota(jnp.int32, (2 * FINE, width), 1)
    wide = jnp.where(wide < 2 * modes, wide, 2 * (wide - 2 * modes))
    by_cos = spread_by(sums, jnp.where(tall == (wide & (FINE - 1)), 1.0, 0.0))
    by_sin = spread_by(sums, jnp.where(tall - FINE == (wide & (FINE - 1)), 1.0, 0.0))
    one, two = groups, 2 * groups
    real = by_cos[:last] - by_sin[last:]
    imaginary = by_cos[last:] + by_sin[:last]
    lane = lax.broadcasted_iota(jnp.int32, (groups, width), 1)
    lane = jnp.where(lane < 2 * modes, lane, 2 * (lane - 2 * modes))
    keep = jnp.where(lane // FINE == lax.broadcasted_iota(jnp.int32, (groups, width), 0), 1.0, 0.0)

    def flat(value):
        return jnp.sum(value * keep[: value.shape[0]], axis=0, keepdims=True)

    near_cos, near_sin = flat(real[:one])[:, : 2 * modes], flat(imaginary[:one])[:, : 2 * modes]
    far_cos, far_sin = flat(real[one:two]), flat(imaginary[one:two])
    info_cos, info_sin = flat(real[two:])[:, :modes], flat(imaginary[two:])[:, :modes]
    info_scale = 1.0 / (OBS_VAR * math.sqrt(modes))
    turn_cos, turn_sin = own_cos * info_scale, own_sin * info_scale
    info = jnp.concatenate(
        [turn_cos * info_cos + turn_sin * info_sin, turn_cos * info_sin - turn_sin * info_cos], axis=1
    )
    square, cross = own_cos * own_cos, own_sin * own_sin
    level = (square + cross) * near_cos[:, modes : modes + 1]
    swing = (square - cross) * far_cos[:, 2 * modes :] + (2.0 * own_cos * own_sin) * far_sin[:, 2 * modes :]
    weight = jnp.concatenate([level + swing, level - swing], axis=1) * (0.5 / (OBS_VAR * modes))
    empty = jnp.zeros((2, 2 * modes), jnp.float32)
    mine[...] = jnp.concatenate(
        [near_cos, near_sin, far_cos[:, : 2 * modes], far_sin[:, : 2 * modes], info, weight, empty], axis=0
    )

    pl.semaphore_wait(barrier, count - 1)
    copies = []
    for offset in range(1, count):
        copy = pltpu.make_async_remote_copy(
            src_ref=mine,
            dst_ref=held.at[offset],
            send_sem=send_sem.at[offset],
            recv_sem=recv_sem.at[offset],
            device_id={tm_axis: lax.rem(own + offset, count)},
            device_id_type=pl.DeviceIdType.MESH,
        )
        copy.start()
        copies.append(copy)
    sums_ref[own] = mine[...]
    for step in range(steps):
        for number in range(2):
            tile_ref[step, number] = jnp.broadcast_to(turn_ref[step, number : number + 1, :], (modes, modes)).T
    for offset in range(1, count):
        copies[offset - 1].wait()
        sums_ref[lax.rem(own + count - offset, count)] = held[offset]


def solve_kernel(
    tm_axis, rows_axis, sums_ref, turn_ref, tile_ref, damp_ref, mean_ref, cov_ref,
    tab, cols, line, fresh, main, full, answer, spare, result,
):
    steps = sums_ref.shape[0]
    width = sums_ref.shape[2]
    modes = width // 2
    block = cov_ref.shape[1]
    own = lax.axis_index(tm_axis)
    block_row = lax.axis_index(rows_axis)
    links = steps - 1
    sides = (slice(0, modes), slice(modes, width))
    damp = damp_ref[0:1, :]
    damp_sq = damp * damp
    lane = lax.broadcasted_iota(jnp.int32, (TILE, modes), 1)
    sub = lax.broadcasted_iota(jnp.int32, (TILE, modes), 0)
    before = jnp.maximum(own - 1, 0)
    inverse_row, flow_row, right_row, info_row, left_row, other_row = range(6)

    def node(i):
        return own if i == links else jnp.where(own > i, i, links - (i - own))

    def load(ref, index, row):
        return tuple(ref[index, row : row + 1, side] for side in sides)

    def note(i, row, values):
        for side, value in zip(sides, values):
            line[i, row : row + 1, side] = value

    past = None
    for i in range(links):
        at = node(i)
        inner = jnp.where(jnp.logical_or(at == 0, at == links), 0.0, 1.0)
        keep = jnp.where(own == i, 0.0, 1.0) if i else 0.0
        level = [1.0 + inner * damp_sq + weight for weight in load(sums_ref, at, 5)]
        if i:
            level = [value - (keep * damp_sq) * old for value, old in zip(level, past)]
        inverse = [1.0 / value for value in level]
        note(i, inverse_row, inverse)
        note(i, right_row, [(keep * damp) * value for value in inverse])
        note(i, info_row, load(sums_ref, at, 4))
        note(i, other_row, [(keep * damp) * old for old in past] if i else [jnp.zeros_like(damp)] * 2)
        for half, value in enumerate(inverse):
            tab[2 * i + half : 2 * i + half + 1, :] = damp * value
        past = inverse
    has_left, has_right = jnp.where(own > 0, 1.0, 0.0), jnp.where(own < links, 1.0, 0.0)
    left, right = load(line, before, inverse_row), past
    level = [
        1.0 + (has_left * has_right) * damp_sq + weight - (has_left * damp_sq) * a - (has_right * damp_sq) * b
        for weight, a, b in zip(load(sums_ref, own, 5), left, right)
    ]
    inverse = [1.0 / value for value in level]
    note(links, inverse_row, inverse)
    note(links, right_row, [damp * value for value in inverse])
    note(links, info_row, load(sums_ref, own, 4))
    left, right = [(has_left * damp) * value for value in left], [(has_right * damp) * value for value in right]
    note(links, left_row, left)
    note(links, other_row, right)
    for half in range(2):
        tab[2 * links + half : 2 * links + half + 1, :] = left[half]
        tab[2 * steps + half : 2 * steps + half + 1, :] = right[half]
    for chunk in range(tab.shape[0] // modes):
        cols[chunk] = tab[chunk * modes : (chunk + 1) * modes, :].T

    def col_of(at, rows):
        value = cols[at // modes, rows, at % modes : at % modes + 1]
        return jnp.broadcast_to(value, (rows.stop - rows.start, modes))

    def build(i):
        at = node(i)
        bases = []
        for row in range(4):
            base = jnp.broadcast_to(sums_ref[at, row : row + 1, :], (TILE, width))
            if row < 2:
                base = pltpu.roll(base, 0, 1, stride=1, stride_axis=0)
                bases.append((base[:, :modes], base[:, modes:]))
            else:
                base = pltpu.roll(base, width - TILE + 1, 1, stride=1, stride_axis=0)
                bases.append([jnp.take_along_axis(base[:, side], TILE - 1 - sub, axis=0) for side in sides])
        turn = [turn_ref[at, k : k + 1, :] for k in range(2)]
        cos_l, sin_l, cos_r, sin_r = [
            jnp.broadcast_to(value * scale, (TILE, modes)) for scale in load(line, i, inverse_row) for value in turn
        ]
        for q in range(modes // TILE):
            shift = TILE * q
            rows = slice(shift, shift + TILE)

            def moved(low, high, edge, amount):
                value = jnp.where(lane >= edge, low, high) if edge else low
                return pltpu.roll(value, amount, 1) if amount % modes else value

            near_cos, near_sin = [
                moved(low, high, modes - shift, shift) if shift else high for low, high in bases[:2]
            ]
            far_cos, far_sin = [moved(low, high, shift, modes - shift) for low, high in bases[2:]]
            up_a, up_b = near_cos + far_cos, far_sin + near_sin
            low_a, low_b = far_sin - near_sin, near_cos - far_cos
            up_left, up_right = up_a * cos_l + up_b * sin_l, up_b * cos_r - up_a * sin_r
            low_left, low_right = low_a * cos_l + low_b * sin_l, low_b * cos_r - low_a * sin_r
            cos_t, sin_t = tile_ref[at, 0, rows, :], tile_ref[at, 1, rows, :]
            off = lane != sub + shift
            under = slice(modes + shift, modes + shift + TILE)
            fresh[i, rows, sides[0]] = jnp.where(off, cos_t * up_left + sin_t * low_left, 0.0)
            fresh[i, rows, sides[1]] = cos_t * up_right + sin_t * low_right
            fresh[i, under, sides[0]] = cos_t * low_left - sin_t * up_left
            fresh[i, under, sides[1]] = jnp.where(off, cos_t * low_right - sin_t * up_right, 0.0)

    pair = 2 * TILE
    strips = [
        (half, slice(start, start + pair), slice(half * modes + start, half * modes + start + pair))
        for half in range(2) for start in range(0, modes, pair)
    ]
    pair_lane = lax.broadcasted_iota(jnp.int32, (pair, modes), 1)
    pair_sub = lax.broadcasted_iota(jnp.int32, (pair, modes), 0)
    ones = jnp.ones((TILE, width), jnp.bfloat16)

    def flow(i, state, third):
        sums = [jnp.zeros((pair, modes), jnp.float32) for _ in sides]
        for half, part, rows in strips:
            parts = []
            for k, side in enumerate(sides):
                value = main[i, rows, side] + third[rows, side]
                full[i, rows, side] = value
                parts.append(value * state[k])
            column = jnp.sum(parts[0] + parts[1], axis=1, keepdims=True)
            sums[half] += jnp.where(pair_lane == pair_sub + part.start, column, 0.0)
        moved = [value - jnp.sum(total, axis=0, keepdims=True) for value, total in zip(state, sums)]
        note(i, flow_row, moved)
        return moved

    def joined(i, old):
        rights = load(line, i, right_row)
        whole = []
        for half, part, rows in strips:
            values = [fresh[i, rows, side] for side in sides]
            if i:
                down = col_of(2 * (i - 1) + half, part)
                values = [value + down * (old[i - 1, rows, side] * right) for value, side, right in zip(values, sides, rights)]
            whole.append(values)
        return whole

    def packed(whole):
        return jnp.concatenate([jnp.concatenate(values, axis=1) for values in whole], axis=0).astype(jnp.bfloat16)

    build(0)
    third, state, most = None, None, jnp.zeros((TILE, width), jnp.float32)
    for i in range(links):
        narrow = packed(joined(i, main))
        square = dot(narrow, narrow)
        if i:
            moved = flow(i - 1, state, third)
            state = [a + b * c for a, b, c in zip(load(line, i, info_row), load(line, i, other_row), moved)]
        else:
            state = load(line, i, info_row)
        build(i + 1)
        for (half, part, rows), values in zip(strips, joined(i, full)):
            for side, value in zip(sides, values):
                main[i, rows, side] = value - square[rows, side]
        squared = square.astype(jnp.bfloat16)
        third = dot(squared, narrow)
        most = jnp.maximum(most, dot(ones, jnp.abs(squared)))
    flow(links - 1, state, third)

    height = block + pair
    tall = lax.broadcasted_iota(jnp.int32, (block, modes), 0)
    wide = lax.broadcasted_iota(jnp.int32, (block, modes), 1)
    hit = wide == (tall + block_row * block) // 2
    even = tall % 2 == 0
    cosines, sines = turn_ref[own, 2:3, :], turn_ref[own, 3:4, :]

    def pose():
        state = [
            a + b * c + d * e
            for a, b, c, d, e in zip(
                load(line, links, info_row), load(line, links, left_row), load(line, before, flow_row),
                load(line, links, other_row), load(line, links - 1, flow_row),
            )
        ]
        scales = load(line, links, inverse_row)
        spare[:block, sides[0]] = jnp.where(hit, jnp.where(even, cosines, sines) * scales[0], 0.0)
        spare[:block, sides[1]] = jnp.where(hit, jnp.where(even, -sines, cosines) * scales[1], 0.0)
        for side, value, scale in zip(sides, state, scales):
            spare[block:, side] = jnp.where(pair_sub == 0, value * scale, 0.0)

    def product(left, right):
        return dot(left[0], right[0]) + (dot(left[0], right[1]) + dot(left[1], right[0]))

    whole = []
    rights = load(line, links, right_row)
    for half, part, rows in strips:
        first, second = col_of(2 * links + half, part), col_of(2 * steps + half, part)
        whole.append([
            fresh[links, rows, side] + (first * full[before, rows, side] + second * full[links - 1, rows, side]) * right
            for side, right in zip(sides, rights)
        ])
    whole = halves(jnp.concatenate([jnp.concatenate(values, axis=1) for values in whole], axis=0))
    square = halves(product(whole, whole))
    pose()
    asked = spare[...]
    first = asked - product(halves(asked), whole)
    fourth = dot(square[0], square[0]).astype(jnp.bfloat16)
    second = first + product(halves(first), square)
    last = dot(ones, jnp.abs(fourth))
    answer[...] = second + dot(second.astype(jnp.bfloat16), fourth)
    good = jnp.logical_and(jnp.max(most) <= CHAIN_BOUND, jnp.max(last) <= LAST_BOUND)

    @pl.when(jnp.logical_not(good))
    def _():
        rows = lax.broadcasted_iota(jnp.int32, (width, width), 0)
        unit = rows == lax.broadcasted_iota(jnp.int32, (width, width), 1)
        source, target = result.at[0], result.at[1]

        def column(row):
            return jnp.sum(jnp.where(unit, row, 0.0), axis=1, keepdims=True)

        def invert(low):
            high = 1.001 * jnp.max(jnp.sum(jnp.abs(source[...]), axis=0, keepdims=True))
            low = jnp.minimum(low, 0.5 * high)
            center = (high + low) / (high - low)
            slope = 2.0 / (high - low)
            top = 2.0 * center * center - 1.0
            target[...] = jnp.where(unit, 4.0 * center * slope / top, 0.0) - (2.0 * slope * slope / top) * source[...]

            def improve(radius):
                factor = 2.0 / (2.0 - radius * radius)
                residue = jnp.where(unit, 1.0, 0.0) - exact(source[...], target[...])
                target[...] = factor * (target[...] + exact(target[...], residue))
                return radius * radius / (2.0 - radius * radius)

            lax.while_loop(lambda radius: radius > TOLERANCE, improve, 1.0 / top)

        def even_out(i, whole):
            root = jnp.sqrt(line[i, inverse_row : inverse_row + 1, :])
            source[...] = jnp.where(unit, 1.0, 0.0) + column(root) * whole * (1.0 / root)
            return root, column(root)

        full[0] = jnp.zeros((width, width), jnp.float32)
        note(0, flow_row, [jnp.zeros_like(damp)] * 2)

        def advance(i, carry):
            old = jnp.maximum(i - 1, 0)
            down = column(line[old, inverse_row : inverse_row + 1, :] * jnp.concatenate([damp, damp], axis=1))
            root, root_col = even_out(i, fresh[i] + down * full[old] * line[i, right_row : right_row + 1, :])
            invert(0.999 * jnp.min(root * root))
            state = line[i, info_row : info_row + 1, :]
            state = state + line[i, other_row : other_row + 1, :] * line[old, flow_row : flow_row + 1, :]
            scaled = jnp.broadcast_to(state * root, (TILE, width))
            line[i, flow_row : flow_row + 1, :] = exact(scaled, target[...])[0:1] * (1.0 / root)
            full[i] = (1.0 / root_col) * (jnp.where(unit, 1.0, 0.0) - target[...]) * root
            return carry

        lax.fori_loop(0, links, advance, 0)
        root, root_col = even_out(
            links,
            fresh[links] + (
                column(line[links, left_row : left_row + 1, :]) * full[before]
                + column(line[links, other_row : other_row + 1, :]) * full[links - 1]
            ) * line[links, right_row : right_row + 1, :],
        )
        invert(0.999 * jnp.min(1.0 - damp_sq) * jnp.min(root * root))
        pose()
        answer[...] = exact(spare[...] * (1.0 / root), target[...]) * root

    left, right = answer[:, sides[0]], answer[:, sides[1]]
    left, right = left * cosines - right * sines, left * sines + right * cosines
    wide = lax.broadcasted_iota(jnp.int32, (height, modes), 1)
    out = []
    for number in range(2):
        pick = wide // 2 + number * (modes // 2)
        out.append(
            jnp.where(wide % 2 == 0, jnp.take_along_axis(left, pick, axis=1), jnp.take_along_axis(right, pick, axis=1))
        )
    for side, value in zip(sides, out):
        cov_ref[0, :, side] = value[:block]
    means = jnp.concatenate([value[block : block + TILE] for value in out], axis=1)
    mean_ref[...] = pltpu.roll(means, width - block_row * block, 1)[0:1, :block]


def local(observations, site_ids, counts, frequencies, decay, proc_var):
    modes = frequencies.shape[0]
    width = 2 * modes
    count = lax.axis_size("tm")
    steps = count * observations.shape[0]
    block = width // lax.axis_size("rows")
    height = block + 2 * TILE
    table = -(-(2 * steps + 2) // modes) * modes
    vmem = pl.BlockSpec(memory_space=pltpu.VMEM)
    smem = pl.BlockSpec(memory_space=pltpu.SMEM)
    hbm = pl.BlockSpec(memory_space=pltpu.HBM)
    shared = pl.pallas_call(
        functools.partial(share_kernel, "tm"),
        out_shape=(
            jax.ShapeDtypeStruct((steps, 8, width), jnp.float32),
            jax.ShapeDtypeStruct((steps, 8, modes), jnp.float32),
            jax.ShapeDtypeStruct((steps, 2, modes, modes), jnp.float32),
            jax.ShapeDtypeStruct((8, modes), jnp.float32),
        ),
        in_specs=[smem] + [hbm] * 5,
        out_specs=(vmem,) * 4,
        scratch_shapes=[
            pltpu.VMEM(site_ids.shape, jnp.int32),
            pltpu.VMEM(observations.shape, jnp.float32),
            pltpu.VMEM((1, modes), jnp.float32),
            pltpu.VMEM((1, modes), jnp.float32),
            pltpu.VMEM((1, modes), jnp.float32),
            pltpu.VMEM((8, width), jnp.float32),
            pltpu.VMEM((count, 8, width), jnp.float32),
            pltpu.SemaphoreType.DMA((5,)),
            pltpu.SemaphoreType.DMA((count,)),
            pltpu.SemaphoreType.DMA((count,)),
        ],
        compiler_params=pltpu.CompilerParams(collective_id=0, has_side_effects=True, vmem_limit_bytes=16 << 20),
        name="share",
    )(
        counts,
        *(
            pltpu.with_memory_space_constraint(value, pltpu.HBM)
            for value in (site_ids, observations, frequencies[None], decay[None], proc_var[None])
        ),
    )
    return pl.pallas_call(
        functools.partial(solve_kernel, "tm", "rows"),
        out_shape=(
            jax.ShapeDtypeStruct((1, block), jnp.float32),
            jax.ShapeDtypeStruct((1, block, width), jnp.float32),
        ),
        in_specs=[vmem] * 4,
        out_specs=(vmem, vmem),
        scratch_shapes=[
            pltpu.VMEM((table, modes), jnp.float32),
            pltpu.VMEM((table // modes, modes, modes), jnp.float32),
            pltpu.VMEM((steps, 8, width), jnp.float32),
            pltpu.VMEM((steps, width, width), jnp.float32),
            pltpu.VMEM((steps - 1, width, width), jnp.float32),
            pltpu.VMEM((steps - 1, width, width), jnp.float32),
            pltpu.VMEM((height, width), jnp.float32),
            pltpu.VMEM((height, width), jnp.float32),
            pltpu.VMEM((2, width, width), jnp.float32),
        ],
        compiler_params=pltpu.CompilerParams(vmem_limit_bytes=40 << 20),
        name="solve",
    )(*shared)


def solution(mesh):
    return jax.shard_map(
        local,
        mesh=mesh,
        in_specs=(P("tm", None), P("tm", None), P("tm"), P(), P(), P()),
        out_specs=(P("tm", "rows"), P("tm", "rows", None)),
        check_vma=False,
    )
```

time: 18.3 us -> 15.7 us (0.86)
  local copies, waits for them, and re-layouts: 2.06 us -> 0 us
  Pallas kernels: 14.6 us -> 14.2 us
    unnamed x10 -> x0, local copies, waits for them, and re-layouts: 2.06 us -> none
    pallas_call x1, Pallas kernels: 5.42 us -> 4.16 us  [local(): pl.pallas_call(functools.partial(solve_kernel, 'tm', 'rows'), out_shape=(...]
    pallas_call x1, Pallas kernels: 9.21 us -> 10.1 us  [local(): pl.pallas_call(functools.partial(share_kernel, 'tm'), out_shape=(jax.Shap...]
where the time goes in v2:
time: 15.7 us; the launch traced here: 15.5 us
  Pallas kernels  14.2 us (90%)
  between operations  1.28 us (8%)
    pallas_call x1, Pallas kernels, local(): pl.pallas_call(functools.partial(share_kernel, 'tm'), out_shape=(jax.Shap...  10.1 us
    pallas_call x1, Pallas kernels, local(): pl.pallas_call(functools.partial(solve_kernel, 'tm', 'rows'), out_shape=(...  4.16 us

profile of v2, /device:TPU:0, one launch (start us, length us, event | category | flops | bytes accessed | tf_op | source)
XLA Modules:
  0.0 15.5 jit_solution(11193843687142400583)
XLA Ops:
  1.3 10.1 %share.1 = (f32[8,8,256]{2,1,0:T(8,128)S(1)}, f32[8,8,128]{2,1,0:T(8,128)S(1)}, f32[8,2,128,128]{3,2,1,0:T(8,128)S(1)}, f32[8,128]{1,0:T(8,128)S(1)}) custom-call(s32[1]{0:T(128)S(6)} %copy.8.counts_ref, s32[1,2048]{1,0:T(1,128)} %site_hbm.1, f32[1,2048]{1,0:T(1,128)} %obs_hbm.1, f32[1,128]{1,0:T(1,128)} %bitcast.3, f32[1,128]{1,0:T(1,128)} %bitcast.4, ...), custom_call_target="tpu_custom_call" | custom-call | tf_op jit(solution)/shard_map/share/pallas_call | solution.py:474
  11.4 4.2 %solve.1 = (f32[1,64]{1,0:T(1,128)}, f32[1,64,256]{2,1,0:T(8,128)}) custom-call(f32[8,8,256]{2,1,0:T(8,128)S(1)} %get-tuple-element.6.sums_ref, f32[8,8,128]{2,1,0:T(8,128)S(1)} %get-tuple-element.7.turn_ref, f32[8,2,128,128]{3,2,1,0:T(8,128)S(1)} %get-tuple-element.8.tile_ref, f32[8,128]{1,0:T(8,128)S(1)} %get-tuple-element.9.damp_ref), custom_call_target="tpu_custom_call" | custom-call | tf_op jit(solution)/shard_map/solve/pallas_call | solution.py:505

commit v3 on v2

--- a/solution.py
+++ b/solution.py
@@ -57,7 +57,7 @@
 
 def share_kernel(
     tm_axis, counts_ref, site_hbm, obs_hbm, freq_hbm, decay_hbm, var_hbm,
-    sums_ref, turn_ref, tile_ref, damp_ref, site_ref, obs_ref, freq_ref, decay_ref, var_ref,
+    sums_ref, turn_ref, tile_ref, mode_ref, site_ref, obs_ref, freq_ref, decay_ref, var_ref,
     mine, held, load_sem, send_sem, recv_sem,
 ):
     count = lax.axis_size(tm_axis)
@@ -65,21 +65,20 @@
     sites = site_ref.shape[1]
     modes = freq_ref.shape[1]
     steps = sums_ref.shape[0]
+    loads = [
+        pltpu.make_async_copy(source, target, load_sem.at[number])
+        for number, (source, target) in enumerate((
+            (site_hbm, site_ref), (obs_hbm, obs_ref), (freq_hbm, freq_ref), (var_hbm, var_ref), (decay_hbm, decay_ref),
+        ))
+    ]
+    for load in loads:
+        load.start()
     barrier = pltpu.get_barrier_semaphore()
     for offset in range(1, count):
         pl.semaphore_signal(
             barrier, inc=1, device_id={tm_axis: lax.rem(own + offset, count)},
             device_id_type=pl.DeviceIdType.MESH,
         )
-    loads = [
-        pltpu.make_async_copy(source, target, load_sem.at[number])
-        for number, (source, target) in enumerate((
-            (site_hbm, site_ref), (freq_hbm, freq_ref), (obs_hbm, obs_ref),
-            (decay_hbm, decay_ref), (var_hbm, var_ref),
-        ))
-    ]
-    for load in loads:
-        load.start()
     for load in loads:
         load.wait()
 
@@ -90,35 +89,48 @@
     turns = jnp.where(frequency < 0.0, -turns, turns)
     share = turns.astype(jnp.float32)
     reduced = (frequency - share * 1.5703125) - share * (0.5 * math.pi - 1.5703125)
-    cosine, sine = quarter_turn(turns + 4, *circle(reduced))
-    now_cos = jnp.sqrt(var_ref[...])
+    turn_cosine, turn_sine = quarter_turn(turns + 4, *circle(reduced))
+    level = 0.5 / (OBS_VAR * modes)
+    root = math.sqrt(level)
+    variance = var_ref[...]
+    mode_ref[0:1, :] = jnp.exp(-decay_ref[...])
+    now_cos = jnp.sqrt(variance)
     now_sin = jnp.zeros_like(now_cos)
     own_cos, own_sin = now_cos, now_sin
-    root = math.sqrt(0.5 / (OBS_VAR * modes))
     for step in range(steps):
         for number, value in enumerate((now_cos * root, now_sin * root, now_cos, now_sin)):
             turn_ref[step, number : number + 1, :] = value
         own_cos = jnp.where(own == step, now_cos, own_cos)
         own_sin = jnp.where(own == step, now_sin, own_sin)
-        now_cos, now_sin = now_cos * cosine - now_sin * sine, now_cos * sine + now_sin * cosine
-    damp_ref[...] = jnp.broadcast_to(jnp.exp(-decay_ref[...]), damp_ref.shape)
-
-    groups = 2 * modes // FINE
-    total = 2 * groups + groups // 2 + FINE
-    last = total - FINE
-    spot = lax.broadcasted_iota(jnp.int32, (total, sites), 0)
-    exponent = jnp.where(spot < groups, spot * FINE - modes, (spot - groups) * FINE + 2)
-    exponent = jnp.where(spot >= 2 * groups, (spot - 2 * groups) * FINE + 1, exponent)
-    exponent = jnp.where(spot >= last, spot - last, exponent)
-    phase = (exponent * site_ref[...]) & (GRID - 1)
-    quadrant = (phase + GRID // 8) >> int(math.log2(GRID // 4))
-    angle = (phase - quadrant * (GRID // 4)).astype(jnp.float32) * (2.0 * math.pi / GRID)
-    cosines, sines = quarter_turn(quadrant, *circle(angle))
+        now_cos, now_sin = (
+            now_cos * turn_cosine - now_sin * turn_sine, now_cos * turn_sine + now_sin * turn_cosine
+        )
+
+    def wave(stride):
+        exponent = lax.broadcasted_iota(jnp.int32, (TILE, sites), 0) * stride
+        phase = (exponent * site_ref[...]) & (GRID - 1)
+        quadrant = (phase + GRID // 8) >> int(math.log2(GRID // 4))
+        angle = (phase - quadrant * (GRID // 4)).astype(jnp.float32) * (2.0 * math.pi / GRID)
+        return quarter_turn(quadrant, *circle(angle))
+
+    def turned(wave, by):
+        return wave[0] * by[0] - wave[1] * by[1], wave[0] * by[1] + wave[1] * by[0]
+
+    def one(wave, row):
+        return wave[0][row : row + 1], wave[1][row : row + 1]
+
+    fine, coarse = wave(1), wave(FINE)
+    eight = turned(one(fine, 4), one(fine, 4))
+    far = turned(one(coarse, 4), one(coarse, 4))
+    far = turned(far, one(fine, 2))
     slots = lax.broadcasted_iota(jnp.int32, (1, sites), 1)
     weights = jnp.where(slots < counts_ref[0], 1.0, 0.0)
-    scale = jnp.where(spot[:last] < 2 * groups, weights, weights * obs_ref[...])
-    left = jnp.concatenate([cosines[:last] * scale, sines[:last] * scale], axis=0)
-    right = jnp.concatenate([cosines[last:], sines[last:]], axis=0)
+    near = coarse[0] * weights, coarse[1] * weights
+    seen = turned(near, one(fine, 1))
+    tiles = (near, turned(near, one(fine, 2)), turned(near, far), (seen[0] * obs_ref[...], seen[1] * obs_ref[...]))
+    left = jnp.concatenate([tile[0] for tile in tiles] + [tile[1] for tile in tiles], axis=0)
+    upper = turned(fine, eight)
+    right = jnp.concatenate([fine[0], upper[0], fine[1], upper[1]], axis=0)
     left_high, left_low = halves(left)
     right_high, right_low = halves(right)
     beside = functools.partial(
@@ -127,38 +139,46 @@
         preferred_element_type=jnp.float32,
     )
     sums = beside(left_high, right_high) + (beside(left_high, right_low) + beside(left_low, right_high))
-    width = 3 * modes
-    tall = lax.broadcasted_iota(jnp.int32, (2 * FINE, width), 0)
-    wide = lax.broadcasted_iota(jnp.int32, (2 * FINE, width), 1)
-    wide = jnp.where(wide < 2 * modes, wide, 2 * (wide - 2 * modes))
-    by_cos = spread_by(sums, jnp.where(tall == (wide & (FINE - 1)), 1.0, 0.0))
-    by_sin = spread_by(sums, jnp.where(tall - FINE == (wide & (FINE - 1)), 1.0, 0.0))
-    one, two = groups, 2 * groups
-    real = by_cos[:last] - by_sin[last:]
-    imaginary = by_cos[last:] + by_sin[:last]
-    lane = lax.broadcasted_iota(jnp.int32, (groups, width), 1)
-    lane = jnp.where(lane < 2 * modes, lane, 2 * (lane - 2 * modes))
-    keep = jnp.where(lane // FINE == lax.broadcasted_iota(jnp.int32, (groups, width), 0), 1.0, 0.0)
-
-    def flat(value):
-        return jnp.sum(value * keep[: value.shape[0]], axis=0, keepdims=True)
-
-    near_cos, near_sin = flat(real[:one])[:, : 2 * modes], flat(imaginary[:one])[:, : 2 * modes]
-    far_cos, far_sin = flat(real[one:two]), flat(imaginary[one:two])
-    info_cos, info_sin = flat(real[two:])[:, :modes], flat(imaginary[two:])[:, :modes]
+    tall = lax.broadcasted_iota(jnp.int32, (2 * FINE, 6 * modes), 0)
+    wide = lax.broadcasted_iota(jnp.int32, (2 * FINE, 6 * modes), 1)
+    picks = jnp.where(wide < 2 * modes, wide, jnp.where(wide < 4 * modes, 2 * wide, 6 * modes - wide)) & (FINE - 1)
+    spread = spread_by(sums, jnp.where(tall == picks + (FINE * (wide // modes)) % (2 * FINE), 1.0, 0.0))
+    half = left.shape[0] // 2
+    pieces = [spread[:, number * modes : (number + 1) * modes] for number in range(6)]
+    real, even_real, back_real = [pieces[number][:half] - pieces[number + 1][half:] for number in (0, 2, 4)]
+    imaginary, even_imaginary, back_imaginary = [
+        pieces[number][half:] + pieces[number + 1][:half] for number in (0, 2, 4)
+    ]
+    lane = lax.broadcasted_iota(jnp.int32, (TILE, modes), 1)
+    group = lax.broadcasted_iota(jnp.int32, (TILE, modes), 0)
+    keep = jnp.where(lane // FINE == group, 1.0, 0.0)
+    keep_low = jnp.where(2 * lane // FINE == group, 1.0, 0.0)
+    keep_back = jnp.where((modes - lane) // FINE == group, 1.0, 0.0)
+    keep_high = jnp.where(2 * lane // FINE == group + TILE, 1.0, 0.0)
+
+    def tile(value, number):
+        return value[number * TILE : (number + 1) * TILE]
+
+    def flat(value, number, keep=keep):
+        return jnp.sum(tile(value, number) * keep, axis=0, keepdims=True)
+
+    def even(value):
+        return jnp.sum(tile(value, 1) * keep_low + tile(value, 2) * keep_high, axis=0, keepdims=True)
+
     info_scale = 1.0 / (OBS_VAR * math.sqrt(modes))
     turn_cos, turn_sin = own_cos * info_scale, own_sin * info_scale
-    info = jnp.concatenate(
-        [turn_cos * info_cos + turn_sin * info_sin, turn_cos * info_sin - turn_sin * info_cos], axis=1
+    info_cos, info_sin = flat(real, 3), flat(imaginary, 3)
+    near_cos = flat(real, 0)
+    mass = (variance * level) * near_cos[:, 0:1]
+    swing = (own_cos * own_cos - own_sin * own_sin) * level * even(even_real)
+    swing = swing + (own_cos * own_sin) * (2.0 * level) * even(even_imaginary)
+    rows = (
+        near_cos, flat(imaginary, 0), flat(real, 1), flat(real, 2), flat(imaginary, 1), flat(imaginary, 2),
+        turn_cos * info_cos + turn_sin * info_sin, turn_cos * info_sin - turn_sin * info_cos,
+        mass + swing, mass - swing, flat(back_real, 0, keep_back), -flat(back_imaginary, 0, keep_back),
+        jnp.zeros((4, modes), jnp.float32),
     )
-    square, cross = own_cos * own_cos, own_sin * own_sin
-    level = (square + cross) * near_cos[:, modes : modes + 1]
-    swing = (square - cross) * far_cos[:, 2 * modes :] + (2.0 * own_cos * own_sin) * far_sin[:, 2 * modes :]
-    weight = jnp.concatenate([level + swing, level - swing], axis=1) * (0.5 / (OBS_VAR * modes))
-    empty = jnp.zeros((2, 2 * modes), jnp.float32)
-    mine[...] = jnp.concatenate(
-        [near_cos, near_sin, far_cos[:, : 2 * modes], far_sin[:, : 2 * modes], info, weight, empty], axis=0
-    )
+    mine[...] = jnp.concatenate(rows, axis=0)
 
     pl.semaphore_wait(barrier, count - 1)
     copies = []
@@ -183,18 +203,18 @@
 
 
 def solve_kernel(
-    tm_axis, rows_axis, sums_ref, turn_ref, tile_ref, damp_ref, mean_ref, cov_ref,
+    tm_axis, rows_axis, sums_ref, turn_ref, tile_ref, mode_ref, mean_ref, cov_ref,
     tab, cols, line, fresh, main, full, answer, spare, result,
 ):
     steps = sums_ref.shape[0]
-    width = sums_ref.shape[2]
-    modes = width // 2
+    modes = sums_ref.shape[2]
+    width = 2 * modes
     block = cov_ref.shape[1]
     own = lax.axis_index(tm_axis)
     block_row = lax.axis_index(rows_axis)
     links = steps - 1
     sides = (slice(0, modes), slice(modes, width))
-    damp = damp_ref[0:1, :]
+    damp = mode_ref[0:1, :]
     damp_sq = damp * damp
     lane = lax.broadcasted_iota(jnp.int32, (TILE, modes), 1)
     sub = lax.broadcasted_iota(jnp.int32, (TILE, modes), 0)
@@ -207,6 +227,12 @@
     def load(ref, index, row):
         return tuple(ref[index, row : row + 1, side] for side in sides)
 
+    def weights_of(at):
+        return tuple(sums_ref[at, row : row + 1, :] for row in (8, 9))
+
+    def info_of(at):
+        return tuple(sums_ref[at, row : row + 1, :] for row in (6, 7))
+
     def note(i, row, values):
         for side, value in zip(sides, values):
             line[i, row : row + 1, side] = value
@@ -216,13 +242,13 @@
         at = node(i)
         inner = jnp.where(jnp.logical_or(at == 0, at == links), 0.0, 1.0)
         keep = jnp.where(own == i, 0.0, 1.0) if i else 0.0
-        level = [1.0 + inner * damp_sq + weight for weight in load(sums_ref, at, 5)]
+        level = [1.0 + inner * damp_sq + mass for mass in weights_of(at)]
         if i:
             level = [value - (keep * damp_sq) * old for value, old in zip(level, past)]
         inverse = [1.0 / value for value in level]
         note(i, inverse_row, inverse)
         note(i, right_row, [(keep * damp) * value for value in inverse])
-        note(i, info_row, load(sums_ref, at, 4))
+        note(i, info_row, info_of(at))
         note(i, other_row, [(keep * damp) * old for old in past] if i else [jnp.zeros_like(damp)] * 2)
         for half, value in enumerate(inverse):
             tab[2 * i + half : 2 * i + half + 1, :] = damp * value
@@ -230,13 +256,13 @@
     has_left, has_right = jnp.where(own > 0, 1.0, 0.0), jnp.where(own < links, 1.0, 0.0)
     left, right = load(line, before, inverse_row), past
     level = [
-        1.0 + (has_left * has_right) * damp_sq + weight - (has_left * damp_sq) * a - (has_right * damp_sq) * b
-        for weight, a, b in zip(load(sums_ref, own, 5), left, right)
+        1.0 + (has_left * has_right) * damp_sq + mass - (has_left * damp_sq) * a - (has_right * damp_sq) * b
+        for mass, a, b in zip(weights_of(own), left, right)
     ]
     inverse = [1.0 / value for value in level]
     note(links, inverse_row, inverse)
     note(links, right_row, [damp * value for value in inverse])
-    note(links, info_row, load(sums_ref, own, 4))
+    note(links, info_row, info_of(own))
     left, right = [(has_left * damp) * value for value in left], [(has_right * damp) * value for value in right]
     note(links, left_row, left)
     note(links, other_row, right)
@@ -253,14 +279,18 @@
     def build(i):
         at = node(i)
         bases = []
-        for row in range(4):
-            base = jnp.broadcast_to(sums_ref[at, row : row + 1, :], (TILE, width))
-            if row < 2:
-                base = pltpu.roll(base, 0, 1, stride=1, stride_axis=0)
-                bases.append((base[:, :modes], base[:, modes:]))
-            else:
-                base = pltpu.roll(base, width - TILE + 1, 1, stride=1, stride_axis=0)
-                bases.append([jnp.take_along_axis(base[:, side], TILE - 1 - sub, axis=0) for side in sides])
+        for rows in ((10, 0), (11, 1)):
+            base = jnp.concatenate(
+                [jnp.broadcast_to(sums_ref[at, row : row + 1, :], (TILE, modes)) for row in rows], axis=1
+            )
+            base = pltpu.roll(base, 0, 1, stride=1, stride_axis=0)
+            bases.append((base[:, :modes], base[:, modes:]))
+        for row in (2, 4):
+            base = jnp.concatenate(
+                [jnp.broadcast_to(sums_ref[at, row + k : row + k + 1, :], (TILE, modes)) for k in range(2)], axis=1
+            )
+            base = pltpu.roll(base, width - TILE + 1, 1, stride=1, stride_axis=0)
+            bases.append([jnp.take_along_axis(base[:, side], TILE - 1 - sub, axis=0) for side in sides])
         turn = [turn_ref[at, k : k + 1, :] for k in range(2)]
         cos_l, sin_l, cos_r, sin_r = [
             jnp.broadcast_to(value * scale, (TILE, modes)) for scale in load(line, i, inverse_row) for value in turn
@@ -474,7 +504,7 @@
     shared = pl.pallas_call(
         functools.partial(share_kernel, "tm"),
         out_shape=(
-            jax.ShapeDtypeStruct((steps, 8, width), jnp.float32),
+            jax.ShapeDtypeStruct((steps, 2 * TILE, modes), jnp.float32),
             jax.ShapeDtypeStruct((steps, 8, modes), jnp.float32),
             jax.ShapeDtypeStruct((steps, 2, modes, modes), jnp.float32),
             jax.ShapeDtypeStruct((8, modes), jnp.float32),
@@ -487,8 +517,8 @@
             pltpu.VMEM((1, modes), jnp.float32),
             pltpu.VMEM((1, modes), jnp.float32),
             pltpu.VMEM((1, modes), jnp.float32),
-            pltpu.VMEM((8, width), jnp.float32),
-            pltpu.VMEM((count, 8, width), jnp.float32),
+            pltpu.VMEM((2 * TILE, modes), jnp.float32),
+            pltpu.VMEM((count, 2 * TILE, modes), jnp.float32),
             pltpu.SemaphoreType.DMA((5,)),
             pltpu.SemaphoreType.DMA((count,)),
             pltpu.SemaphoreType.DMA((count,)),

time: 15.7 us -> 15.2 us (0.968)
  Pallas kernels: 14.2 us -> 13.7 us
    pallas_call x1, Pallas kernels: 10.1 us -> 9.51 us  [local(): pl.pallas_call(functools.partial(share_kernel, 'tm'), out_shape=(jax.Shap...]
where the time goes in v3:
time: 15.2 us; the launch traced here: 14.9 us
  Pallas kernels  13.7 us (90%)
  between operations  1.28 us (8%)
    pallas_call x1, Pallas kernels, local(): pl.pallas_call(functools.partial(share_kernel, 'tm'), out_shape=(jax.Shap...  9.51 us
    pallas_call x1, Pallas kernels, local(): pl.pallas_call(functools.partial(solve_kernel, 'tm', 'rows'), out_shape=(...  4.15 us

profile of v3, /device:TPU:0, one launch (start us, length us, event | category | flops | bytes accessed | tf_op | source)
XLA Modules:
  0.0 14.9 jit_solution(3758955848366604738)
XLA Ops:
  1.3 9.5 %share.1 = (f32[8,16,128]{2,1,0:T(8,128)S(1)}, f32[8,8,128]{2,1,0:T(8,128)S(1)}, f32[8,2,128,128]{3,2,1,0:T(8,128)S(1)}, f32[8,128]{1,0:T(8,128)S(1)}) custom-call(s32[1]{0:T(128)S(6)} %copy.8.counts_ref, s32[1,2048]{1,0:T(1,128)} %site_hbm.1, f32[1,2048]{1,0:T(1,128)} %obs_hbm.1, f32[1,128]{1,0:T(1,128)} %bitcast.3, f32[1,128]{1,0:T(1,128)} %bitcast.4, ...), custom_call_target="tpu_custom_call" | custom-call | tf_op jit(solution)/shard_map/share/pallas_call | solution.py:504
  10.8 4.1 %solve.1 = (f32[1,64]{1,0:T(1,128)}, f32[1,64,256]{2,1,0:T(8,128)}) custom-call(f32[8,16,128]{2,1,0:T(8,128)S(1)} %get-tuple-element.6.sums_ref, f32[8,8,128]{2,1,0:T(8,128)S(1)} %get-tuple-element.7.turn_ref, f32[8,2,128,128]{3,2,1,0:T(8,128)S(1)} %get-tuple-element.8.tile_ref, f32[8,128]{1,0:T(8,128)S(1)} %get-tuple-element.9.mode_ref), custom_call_target="tpu_custom_call" | custom-call | tf_op jit(solution)/shard_map/solve/pallas_call | solution.py:535

commit v4 on v3

--- a/solution.py
+++ b/solution.py
@@ -12,9 +12,17 @@
 OBS_VAR = 64
 FINE = 16
 TILE = 8
+LANES = 128
 CHAIN_BOUND = 2.5e-3
 LAST_BOUND = 5e-3
 TOLERANCE = 1e-6
+HALF_UNIT = math.pi / GRID
+HALF_SINE = tuple(-2.0 * c * HALF_UNIT ** (2 * k + 1) for k, c in enumerate((
+    0.9999999766, -0.1666664763, 0.008332899823, -0.0001980089775, 2.590488469e-06
+)))
+HALF_COSINE = tuple(c * HALF_UNIT ** (2 * k) for k, c in enumerate((
+    0.9999999535, -0.4999990535, 0.04166358469, -0.001385370429, 2.315393125e-05
+)))
 
 exact_mode = lax.Precision.HIGHEST
 
@@ -57,12 +65,11 @@
 
 def share_kernel(
     tm_axis, counts_ref, site_hbm, obs_hbm, freq_hbm, decay_hbm, var_hbm,
-    sums_ref, turn_ref, tile_ref, mode_ref, site_ref, obs_ref, freq_ref, decay_ref, var_ref,
-    mine, held, load_sem, send_sem, recv_sem,
+    sums_ref, turn_ref, fresh_ref, mode_ref, site_ref, obs_ref, freq_ref, decay_ref, var_ref,
+    tile_ref, factor_ref, mine, held, load_sem, send_sem, recv_sem,
 ):
     count = lax.axis_size(tm_axis)
     own = lax.axis_index(tm_axis)
-    sites = site_ref.shape[1]
     modes = freq_ref.shape[1]
     steps = sums_ref.shape[0]
     loads = [
@@ -106,31 +113,44 @@
             now_cos * turn_cosine - now_sin * turn_sine, now_cos * turn_sine + now_sin * turn_cosine
         )
 
-    def wave(stride):
-        exponent = lax.broadcasted_iota(jnp.int32, (TILE, sites), 0) * stride
-        phase = (exponent * site_ref[...]) & (GRID - 1)
-        quadrant = (phase + GRID // 8) >> int(math.log2(GRID // 4))
-        angle = (phase - quadrant * (GRID // 4)).astype(jnp.float32) * (2.0 * math.pi / GRID)
-        return quarter_turn(quadrant, *circle(angle))
+    rows, lanes = site_ref.shape
+    half_turn = GRID // 2
+    place = lax.broadcasted_iota(jnp.int32, (TILE, lanes), 0)
+
+    def wave(sites, exponent):
+        at = ((exponent * sites) & (GRID - 1)).astype(jnp.float32) - half_turn
+        square = at * at
+        sine, cosine = HALF_SINE[-1], HALF_COSINE[-1]
+        for a in HALF_SINE[-2::-1]:
+            sine = sine * square + a
+        for a in HALF_COSINE[-2::-1]:
+            cosine = cosine * square + a
+        sine = sine * at
+        return (sine * sine) * 0.5 - 1.0, sine * cosine
 
     def turned(wave, by):
         return wave[0] * by[0] - wave[1] * by[1], wave[0] * by[1] + wave[1] * by[0]
 
-    def one(wave, row):
-        return wave[0][row : row + 1], wave[1][row : row + 1]
-
-    fine, coarse = wave(1), wave(FINE)
-    eight = turned(one(fine, 4), one(fine, 4))
-    far = turned(one(coarse, 4), one(coarse, 4))
-    far = turned(far, one(fine, 2))
-    slots = lax.broadcasted_iota(jnp.int32, (1, sites), 1)
-    weights = jnp.where(slots < counts_ref[0], 1.0, 0.0)
-    near = coarse[0] * weights, coarse[1] * weights
-    seen = turned(near, one(fine, 1))
-    tiles = (near, turned(near, one(fine, 2)), turned(near, far), (seen[0] * obs_ref[...], seen[1] * obs_ref[...]))
-    left = jnp.concatenate([tile[0] for tile in tiles] + [tile[1] for tile in tiles], axis=0)
-    upper = turned(fine, eight)
-    right = jnp.concatenate([fine[0], upper[0], fine[1], upper[1]], axis=0)
+    sites = site_ref[...]
+    one = wave(sites, 1)
+    two = turned(one, one)
+    far = turned(wave(sites, FINE * TILE), two)
+    slots = lax.broadcasted_iota(jnp.int32, (rows, lanes), 0) * lanes + lax.broadcasted_iota(jnp.int32, (rows, lanes), 1)
+    live = jnp.where(slots < counts_ref[0], 1.0, 0.0)
+    seen = live * obs_ref[...]
+    factors = (live, *[v * live for v in two], *[v * live for v in far], *[v * seen for v in one], *wave(sites, TILE))
+    for number, value in enumerate(factors):
+        factor_ref[number] = value
+    left, right = [], []
+    for row in range(rows):
+        spot = jnp.broadcast_to(site_ref[row : row + 1, :], (TILE, lanes))
+        fine, coarse = wave(spot, place), wave(spot, place * FINE)
+        live, *by = [jnp.broadcast_to(factor_ref[k, row : row + 1, :], (TILE, lanes)) for k in range(len(factors))]
+        tiles = [(coarse[0] * live, coarse[1] * live)] + [turned(coarse, by[k : k + 2]) for k in (0, 2, 4)]
+        upper = turned(fine, by[6:8])
+        left.append(jnp.concatenate([tile[0] for tile in tiles] + [tile[1] for tile in tiles], axis=0))
+        right.append(jnp.concatenate([fine[0], upper[0], fine[1], upper[1]], axis=0))
+    left, right = jnp.concatenate(left, axis=1), jnp.concatenate(right, axis=1)
     left_high, left_low = halves(left)
     right_high, right_low = halves(right)
     beside = functools.partial(
@@ -193,18 +213,79 @@
         )
         copy.start()
         copies.append(copy)
-    sums_ref[own] = mine[...]
     for step in range(steps):
         for number in range(2):
             tile_ref[step, number] = jnp.broadcast_to(turn_ref[step, number : number + 1, :], (modes, modes)).T
-    for offset in range(1, count):
-        copies[offset - 1].wait()
-        sums_ref[lax.rem(own + count - offset, count)] = held[offset]
+
+    sub = group
+
+    def build(at, message):
+        bases = []
+        for numbers in ((10, 0), (11, 1), (2, 3), (4, 5)):
+            base = jnp.concatenate(
+                [jnp.broadcast_to(message[number : number + 1, :], (TILE, modes)) for number in numbers], axis=1
+            )
+            if numbers[0] >= FINE // 2 + 2:
+                base = pltpu.roll(base, 0, 1, stride=1, stride_axis=0)
+                bases.append((base[:, :modes], base[:, modes:]))
+            else:
+                base = pltpu.roll(base, 2 * modes - TILE + 1, 1, stride=1, stride_axis=0)
+                bases.append([
+                    jnp.take_along_axis(base[:, k * modes : (k + 1) * modes], TILE - 1 - sub, axis=0) for k in range(2)
+                ])
+        cos_c, sin_c = [jnp.broadcast_to(turn_ref[at, k : k + 1, :], (TILE, modes)) for k in range(2)]
+        for q in range(modes // TILE):
+            shift = TILE * q
+            spots = slice(shift, shift + TILE)
+
+            def moved(low, high, edge, amount):
+                value = jnp.where(lane >= edge, low, high) if edge else low
+                return pltpu.roll(value, amount, 1) if amount % modes else value
+
+            near_cos, near_sin = [
+                moved(low, high, modes - shift, shift) if shift else high for low, high in bases[:2]
+            ]
+            far_cos, far_sin = [moved(low, high, shift, modes - shift) for low, high in bases[2:]]
+            up_a, up_b = near_cos + far_cos, far_sin + near_sin
+            low_a, low_b = far_sin - near_sin, near_cos - far_cos
+            up_left, up_right = up_a * cos_c + up_b * sin_c, up_b * cos_c - up_a * sin_c
+            low_left, low_right = low_a * cos_c + low_b * sin_c, low_b * cos_c - low_a * sin_c
+            cos_t, sin_t = tile_ref[at, 0, spots, :], tile_ref[at, 1, spots, :]
+            off = lane != sub + shift
+            under = slice(modes + shift, modes + shift + TILE)
+            fresh_ref[at, spots, :modes] = jnp.where(off, cos_t * up_left + sin_t * low_left, 0.0)
+            fresh_ref[at, spots, modes:] = cos_t * up_right + sin_t * low_right
+            fresh_ref[at, under, :modes] = cos_t * low_left - sin_t * up_left
+            fresh_ref[at, under, modes:] = jnp.where(off, cos_t * low_right - sin_t * up_right, 0.0)
+
+    def take(number, carry):
+        offset = count - 1 - number
+        arrived = pltpu.make_async_remote_copy(
+            src_ref=mine,
+            dst_ref=held.at[offset],
+            send_sem=send_sem.at[offset],
+            recv_sem=recv_sem.at[offset],
+            device_id={tm_axis: lax.rem(own + offset, count)},
+            device_id_type=pl.DeviceIdType.MESH,
+        )
+        arrived.wait_recv()
+        peer = lax.rem(own + count - offset, count)
+        message = held[offset]
+        sums_ref[peer] = message
+        build(peer, message)
+        return carry
+
+    message = mine[...]
+    sums_ref[own] = message
+    build(own, message)
+    lax.fori_loop(0, count - 1, take, 0)
+    for copy in copies:
+        copy.wait_send()
 
 
 def solve_kernel(
-    tm_axis, rows_axis, sums_ref, turn_ref, tile_ref, mode_ref, mean_ref, cov_ref,
-    tab, cols, line, fresh, main, full, answer, spare, result,
+    tm_axis, rows_axis, sums_ref, turn_ref, fresh, mode_ref, mean_ref, cov_ref,
+    tab, cols, line, kept, main, full, answer, spare, result,
 ):
     steps = sums_ref.shape[0]
     modes = sums_ref.shape[2]
@@ -276,49 +357,6 @@
         value = cols[at // modes, rows, at % modes : at % modes + 1]
         return jnp.broadcast_to(value, (rows.stop - rows.start, modes))
 
-    def build(i):
-        at = node(i)
-        bases = []
-        for rows in ((10, 0), (11, 1)):
-            base = jnp.concatenate(
-                [jnp.broadcast_to(sums_ref[at, row : row + 1, :], (TILE, modes)) for row in rows], axis=1
-            )
-            base = pltpu.roll(base, 0, 1, stride=1, stride_axis=0)
-            bases.append((base[:, :modes], base[:, modes:]))
-        for row in (2, 4):
-            base = jnp.concatenate(
-                [jnp.broadcast_to(sums_ref[at, row + k : row + k + 1, :], (TILE, modes)) for k in range(2)], axis=1
-            )
-            base = pltpu.roll(base, width - TILE + 1, 1, stride=1, stride_axis=0)
-            bases.append([jnp.take_along_axis(base[:, side], TILE - 1 - sub, axis=0) for side in sides])
-        turn = [turn_ref[at, k : k + 1, :] for k in range(2)]
-        cos_l, sin_l, cos_r, sin_r = [
-            jnp.broadcast_to(value * scale, (TILE, modes)) for scale in load(line, i, inverse_row) for value in turn
-        ]
-        for q in range(modes // TILE):
-            shift = TILE * q
-            rows = slice(shift, shift + TILE)
-
-            def moved(low, high, edge, amount):
-                value = jnp.where(lane >= edge, low, high) if edge else low
-                return pltpu.roll(value, amount, 1) if amount % modes else value
-
-            near_cos, near_sin = [
-                moved(low, high, modes - shift, shift) if shift else high for low, high in bases[:2]
-            ]
-            far_cos, far_sin = [moved(low, high, shift, modes - shift) for low, high in bases[2:]]
-            up_a, up_b = near_cos + far_cos, far_sin + near_sin
-            low_a, low_b = far_sin - near_sin, near_cos - far_cos
-            up_left, up_right = up_a * cos_l + up_b * sin_l, up_b * cos_r - up_a * sin_r
-            low_left, low_right = low_a * cos_l + low_b * sin_l, low_b * cos_r - low_a * sin_r
-            cos_t, sin_t = tile_ref[at, 0, rows, :], tile_ref[at, 1, rows, :]
-            off = lane != sub + shift
-            under = slice(modes + shift, modes + shift + TILE)
-            fresh[i, rows, sides[0]] = jnp.where(off, cos_t * up_left + sin_t * low_left, 0.0)
-            fresh[i, rows, sides[1]] = cos_t * up_right + sin_t * low_right
-            fresh[i, under, sides[0]] = cos_t * low_left - sin_t * up_left
-            fresh[i, under, sides[1]] = jnp.where(off, cos_t * low_right - sin_t * up_right, 0.0)
-
     pair = 2 * TILE
     strips = [
         (half, slice(start, start + pair), slice(half * modes + start, half * modes + start + pair))
@@ -342,34 +380,36 @@
         note(i, flow_row, moved)
         return moved
 
-    def joined(i, old):
-        rights = load(line, i, right_row)
-        whole = []
-        for half, part, rows in strips:
-            values = [fresh[i, rows, side] for side in sides]
-            if i:
-                down = col_of(2 * (i - 1) + half, part)
-                values = [value + down * (old[i - 1, rows, side] * right) for value, side, right in zip(values, sides, rights)]
-            whole.append(values)
-        return whole
-
     def packed(whole):
         return jnp.concatenate([jnp.concatenate(values, axis=1) for values in whole], axis=0).astype(jnp.bfloat16)
 
-    build(0)
     third, state, most = None, None, jnp.zeros((TILE, width), jnp.float32)
     for i in range(links):
-        narrow = packed(joined(i, main))
+        scales, rights = load(line, i, inverse_row), load(line, i, right_row)
+        downs = [col_of(2 * (i - 1) + half, part) for half, part, rows in strips] if i else [None] * len(strips)
+        whole = []
+        for (half, part, rows), down in zip(strips, downs):
+            values = []
+            for side, scale, right in zip(sides, scales, rights):
+                value = fresh[node(i), rows, side] * scale
+                if i:
+                    value = value + down * (main[i - 1, rows, side] * right)
+                kept[i % 2, rows, side] = value
+                values.append(value)
+            whole.append(values)
+        narrow = packed(whole)
         square = dot(narrow, narrow)
         if i:
             moved = flow(i - 1, state, third)
             state = [a + b * c for a, b, c in zip(load(line, i, info_row), load(line, i, other_row), moved)]
         else:
             state = load(line, i, info_row)
-        build(i + 1)
-        for (half, part, rows), values in zip(strips, joined(i, full)):
-            for side, value in zip(sides, values):
-                main[i, rows, side] = value - square[rows, side]
+        for (half, part, rows), down in zip(strips, downs):
+            for side, right in zip(sides, rights):
+                value = kept[i % 2, rows, side] - square[rows, side]
+                if i:
+                    value = value + down * (third[rows, side] * right)
+                main[i, rows, side] = value
         squared = square.astype(jnp.bfloat16)
         third = dot(squared, narrow)
         most = jnp.maximum(most, dot(ones, jnp.abs(squared)))
@@ -400,12 +440,12 @@
         return dot(left[0], right[0]) + (dot(left[0], right[1]) + dot(left[1], right[0]))
 
     whole = []
-    rights = load(line, links, right_row)
+    scales, rights = load(line, links, inverse_row), load(line, links, right_row)
     for half, part, rows in strips:
         first, second = col_of(2 * links + half, part), col_of(2 * steps + half, part)
         whole.append([
-            fresh[links, rows, side] + (first * full[before, rows, side] + second * full[links - 1, rows, side]) * right
-            for side, right in zip(sides, rights)
+            fresh[own, rows, side] * scale + (first * full[before, rows, side] + second * full[links - 1, rows, side]) * right
+            for side, scale, right in zip(sides, scales, rights)
         ])
     whole = halves(jnp.concatenate([jnp.concatenate(values, axis=1) for values in whole], axis=0))
     square = halves(product(whole, whole))
@@ -454,7 +494,9 @@
         def advance(i, carry):
             old = jnp.maximum(i - 1, 0)
             down = column(line[old, inverse_row : inverse_row + 1, :] * jnp.concatenate([damp, damp], axis=1))
-            root, root_col = even_out(i, fresh[i] + down * full[old] * line[i, right_row : right_row + 1, :])
+            at = jnp.where(own > i, i, links - (i - own))
+            plain = fresh[at] * line[i, inverse_row : inverse_row + 1, :]
+            root, root_col = even_out(i, plain + down * full[old] * line[i, right_row : right_row + 1, :])
             invert(0.999 * jnp.min(root * root))
             state = line[i, info_row : info_row + 1, :]
             state = state + line[i, other_row : other_row + 1, :] * line[old, flow_row : flow_row + 1, :]
@@ -466,7 +508,7 @@
         lax.fori_loop(0, links, advance, 0)
         root, root_col = even_out(
             links,
-            fresh[links] + (
+            fresh[own] * line[links, inverse_row : inverse_row + 1, :] + (
                 column(line[links, left_row : left_row + 1, :]) * full[before]
                 + column(line[links, other_row : other_row + 1, :]) * full[links - 1]
             ) * line[links, right_row : right_row + 1, :],
@@ -497,6 +539,7 @@
     steps = count * observations.shape[0]
     block = width // lax.axis_size("rows")
     height = block + 2 * TILE
+    dense = (site_ids.shape[1] // LANES, LANES)
     table = -(-(2 * steps + 2) // modes) * modes
     vmem = pl.BlockSpec(memory_space=pltpu.VMEM)
     smem = pl.BlockSpec(memory_space=pltpu.SMEM)
@@ -506,17 +549,19 @@
         out_shape=(
             jax.ShapeDtypeStruct((steps, 2 * TILE, modes), jnp.float32),
             jax.ShapeDtypeStruct((steps, 8, modes), jnp.float32),
-            jax.ShapeDtypeStruct((steps, 2, modes, modes), jnp.float32),
+            jax.ShapeDtypeStruct((steps, width, width), jnp.float32),
             jax.ShapeDtypeStruct((8, modes), jnp.float32),
         ),
         in_specs=[smem] + [hbm] * 5,
         out_specs=(vmem,) * 4,
         scratch_shapes=[
-            pltpu.VMEM(site_ids.shape, jnp.int32),
-            pltpu.VMEM(observations.shape, jnp.float32),
+            pltpu.VMEM(dense, jnp.int32),
+            pltpu.VMEM(dense, jnp.float32),
             pltpu.VMEM((1, modes), jnp.float32),
             pltpu.VMEM((1, modes), jnp.float32),
             pltpu.VMEM((1, modes), jnp.float32),
+            pltpu.VMEM((steps, 2, modes, modes), jnp.float32),
+            pltpu.VMEM((9, *dense), jnp.float32),
             pltpu.VMEM((2 * TILE, modes), jnp.float32),
             pltpu.VMEM((count, 2 * TILE, modes), jnp.float32),
             pltpu.SemaphoreType.DMA((5,)),
@@ -529,7 +574,7 @@
         counts,
         *(
             pltpu.with_memory_space_constraint(value, pltpu.HBM)
-            for value in (site_ids, observations, frequencies[None], decay[None], proc_var[None])
+            for value in (site_ids.reshape(dense), observations.reshape(dense), frequencies[None], decay[None], proc_var[None])
         ),
     )
     return pl.pallas_call(
@@ -544,7 +589,7 @@
             pltpu.VMEM((table, modes), jnp.float32),
             pltpu.VMEM((table // modes, modes, modes), jnp.float32),
             pltpu.VMEM((steps, 8, width), jnp.float32),
-            pltpu.VMEM((steps, width, width), jnp.float32),
+            pltpu.VMEM((2, width, width), jnp.float32),
             pltpu.VMEM((steps - 1, width, width), jnp.float32),
             pltpu.VMEM((steps - 1, width, width), jnp.float32),
             pltpu.VMEM((height, width), jnp.float32),

time: 15.2 us -> 14.9 us (0.980)
  Pallas kernels: 13.7 us -> 13.4 us
    pallas_call x1, Pallas kernels: 4.15 us -> 3.3 us  [local(): pl.pallas_call(functools.partial(solve_kernel, 'tm', 'rows'), out_shape=(...]
    pallas_call x1, Pallas kernels: 9.51 us -> 10.1 us  [local(): pl.pallas_call(functools.partial(share_kernel, 'tm'), out_shape=(jax.Shap...]
where the time goes in v4:
time: 14.9 us; the launch traced here: 14.7 us
  Pallas kernels  13.4 us (90%)
  between operations  1.28 us (9%)
    pallas_call x1, Pallas kernels, local(): pl.pallas_call(functools.partial(share_kernel, 'tm'), out_shape=(jax.Shap...  10.1 us
    pallas_call x1, Pallas kernels, local(): pl.pallas_call(functools.partial(solve_kernel, 'tm', 'rows'), out_shape=(...  3.3 us

profile of v4, /device:TPU:0, one launch (start us, length us, event | category | flops | bytes accessed | tf_op | source)
XLA Modules:
  0.0 14.7 jit_solution(6980966851439678241)
XLA Ops:
  1.3 10.1 %share.1 = (f32[8,16,128]{2,1,0:T(8,128)S(1)}, f32[8,8,128]{2,1,0:T(8,128)S(1)}, f32[8,256,256]{2,1,0:T(8,128)S(1)}, f32[8,128]{1,0:T(8,128)S(1)}) custom-call(s32[1]{0:T(128)S(6)} %copy.8.counts_ref, s32[16,128]{1,0:T(8,128)} %bitcast.5, f32[16,128]{1,0:T(8,128)} %bitcast.6, f32[1,128]{1,0:T(1,128)} %bitcast.7, f32[1,128]{1,0:T(1,128)} %bitcast.8, ...), custom_call_target="tpu_custom_call" | custom-call | tf_op jit(solution)/shard_map/share/pallas_call | solution.py:547
  11.4 3.3 %solve.1 = (f32[1,64]{1,0:T(1,128)}, f32[1,64,256]{2,1,0:T(8,128)}) custom-call(f32[8,16,128]{2,1,0:T(8,128)S(1)} %get-tuple-element.6.sums_ref, f32[8,8,128]{2,1,0:T(8,128)S(1)} %get-tuple-element.7.turn_ref, f32[8,256,256]{2,1,0:T(8,128)S(1)} %get-tuple-element.8.fresh, f32[8,128]{1,0:T(8,128)S(1)} %get-tuple-element.9.mode_ref), custom_call_target="tpu_custom_call" | custom-call | tf_op jit(solution)/shard_map/solve/pallas_call | solution.py:580

commit v5 on v4

--- a/solution.py
+++ b/solution.py
@@ -258,27 +258,35 @@
             fresh_ref[at, under, :modes] = cos_t * low_left - sin_t * up_left
             fresh_ref[at, under, modes:] = jnp.where(off, cos_t * low_right - sin_t * up_right, 0.0)
 
-    def take(number, carry):
-        offset = count - 1 - number
-        arrived = pltpu.make_async_remote_copy(
+    def arrive(offset):
+        pltpu.make_async_remote_copy(
             src_ref=mine,
             dst_ref=held.at[offset],
             send_sem=send_sem.at[offset],
             recv_sem=recv_sem.at[offset],
             device_id={tm_axis: lax.rem(own + offset, count)},
             device_id_type=pl.DeviceIdType.MESH,
-        )
-        arrived.wait_recv()
-        peer = lax.rem(own + count - offset, count)
-        message = held[offset]
-        sums_ref[peer] = message
-        build(peer, message)
+        ).wait_recv()
+
+    def take(offsets):
+        for offset in offsets:
+            arrive(offset)
+        for offset in offsets:
+            peer = lax.rem(own + count - offset, count)
+            message = held[offset]
+            sums_ref[peer] = message
+            build(peer, message)
+
+    def take_two(number, carry):
+        take((count - 1 - 2 * number, count - 2 - 2 * number))
         return carry
 
     message = mine[...]
     sums_ref[own] = message
     build(own, message)
-    lax.fori_loop(0, count - 1, take, 0)
+    lax.fori_loop(0, (count - 1) // 2, take_two, 0)
+    if (count - 1) % 2:
+        take((1,))
     for copy in copies:
         copy.wait_send()
 
@@ -448,14 +456,16 @@
             for side, scale, right in zip(sides, scales, rights)
         ])
     whole = halves(jnp.concatenate([jnp.concatenate(values, axis=1) for values in whole], axis=0))
-    square = halves(product(whole, whole))
     pose()
     asked = spare[...]
-    first = asked - product(halves(asked), whole)
-    fourth = dot(square[0], square[0]).astype(jnp.bfloat16)
-    second = first + product(halves(first), square)
+    first = product(halves(asked), whole)
+    square = dot(whole[0], whole[0]).astype(jnp.bfloat16)
+    second = product(halves(first), whole)
+    fourth = dot(square, square).astype(jnp.bfloat16)
+    third = dot(second.astype(jnp.bfloat16), whole[0])
     last = dot(ones, jnp.abs(fourth))
-    answer[...] = second + dot(second.astype(jnp.bfloat16), fourth)
+    reached = (asked - first) + (second - third)
+    answer[...] = reached + dot(reached.astype(jnp.bfloat16), fourth)
     good = jnp.logical_and(jnp.max(most) <= CHAIN_BOUND, jnp.max(last) <= LAST_BOUND)
 
     @pl.when(jnp.logical_not(good))

time: 14.9 us -> 14.3 us (0.960)
  Pallas kernels: 13.4 us -> 12.8 us
    pallas_call x1, Pallas kernels: 10.1 us -> 9.63 us  [local(): pl.pallas_call(functools.partial(share_kernel, 'tm'), out_shape=(jax.Shap...]
where the time goes in v5:
time: 14.3 us; the launch traced here: 14.1 us
  Pallas kernels  12.8 us (90%)
  between operations  1.28 us (9%)
    pallas_call x1, Pallas kernels, local(): pl.pallas_call(functools.partial(share_kernel, 'tm'), out_shape=(jax.Shap...  9.63 us
    pallas_call x1, Pallas kernels, local(): pl.pallas_call(functools.partial(solve_kernel, 'tm', 'rows'), out_shape=(...  3.22 us

profile of v5, /device:TPU:0, one launch (start us, length us, event | category | flops | bytes accessed | tf_op | source)
XLA Modules:
  0.0 14.1 jit_solution(13032821467248828502)
XLA Ops:
  1.3 9.6 %share.1 = (f32[8,16,128]{2,1,0:T(8,128)S(1)}, f32[8,8,128]{2,1,0:T(8,128)S(1)}, f32[8,256,256]{2,1,0:T(8,128)S(1)}, f32[8,128]{1,0:T(8,128)S(1)}) custom-call(s32[1]{0:T(128)S(6)} %copy.8.counts_ref, s32[16,128]{1,0:T(8,128)} %bitcast.5, f32[16,128]{1,0:T(8,128)} %bitcast.6, f32[1,128]{1,0:T(1,128)} %bitcast.7, f32[1,128]{1,0:T(1,128)} %bitcast.8, ...), custom_call_target="tpu_custom_call" | custom-call | tf_op jit(solution)/shard_map/share/pallas_call | solution.py:557
  10.9 3.2 %solve.1 = (f32[1,64]{1,0:T(1,128)}, f32[1,64,256]{2,1,0:T(8,128)}) custom-call(f32[8,16,128]{2,1,0:T(8,128)S(1)} %get-tuple-element.6.sums_ref, f32[8,8,128]{2,1,0:T(8,128)S(1)} %get-tuple-element.7.turn_ref, f32[8,256,256]{2,1,0:T(8,128)S(1)} %get-tuple-element.8.fresh, f32[8,128]{1,0:T(8,128)S(1)} %get-tuple-element.9.mode_ref), custom_call_target="tpu_custom_call" | custom-call | tf_op jit(solution)/shard_map/solve/pallas_call | solution.py:590

commit v6 on v5

--- a/solution.py
+++ b/solution.py
@@ -456,10 +456,10 @@
             for side, scale, right in zip(sides, scales, rights)
         ])
     whole = halves(jnp.concatenate([jnp.concatenate(values, axis=1) for values in whole], axis=0))
+    square = dot(whole[0], whole[0]).astype(jnp.bfloat16)
     pose()
     asked = spare[...]
     first = product(halves(asked), whole)
-    square = dot(whole[0], whole[0]).astype(jnp.bfloat16)
     second = product(halves(first), whole)
     fourth = dot(square, square).astype(jnp.bfloat16)
     third = dot(second.astype(jnp.bfloat16), whole[0])

time: 14.3 us -> 14.3 us (level)
  no operation moved by 1% of the time
where the time goes in v6:
time: 14.3 us; the launch traced here: 14.1 us
  Pallas kernels  12.8 us (90%)
  between operations  1.28 us (9%)
    pallas_call x1, Pallas kernels, local(): pl.pallas_call(functools.partial(share_kernel, 'tm'), out_shape=(jax.Shap...  9.63 us
    pallas_call x1, Pallas kernels, local(): pl.pallas_call(functools.partial(solve_kernel, 'tm', 'rows'), out_shape=(...  3.21 us

profile of v6, /device:TPU:0, one launch (start us, length us, event | category | flops | bytes accessed | tf_op | source)
XLA Modules:
  0.0 14.1 jit_solution(10728941532976148839)
XLA Ops:
  1.3 9.6 %share.1 = (f32[8,16,128]{2,1,0:T(8,128)S(1)}, f32[8,8,128]{2,1,0:T(8,128)S(1)}, f32[8,256,256]{2,1,0:T(8,128)S(1)}, f32[8,128]{1,0:T(8,128)S(1)}) custom-call(s32[1]{0:T(128)S(6)} %copy.8.counts_ref, s32[16,128]{1,0:T(8,128)} %bitcast.5, f32[16,128]{1,0:T(8,128)} %bitcast.6, f32[1,128]{1,0:T(1,128)} %bitcast.7, f32[1,128]{1,0:T(1,128)} %bitcast.8, ...), custom_call_target="tpu_custom_call" | custom-call | tf_op jit(solution)/shard_map/share/pallas_call | solution.py:557
  10.9 3.2 %solve.1 = (f32[1,64]{1,0:T(1,128)}, f32[1,64,256]{2,1,0:T(8,128)}) custom-call(f32[8,16,128]{2,1,0:T(8,128)S(1)} %get-tuple-element.6.sums_ref, f32[8,8,128]{2,1,0:T(8,128)S(1)} %get-tuple-element.7.turn_ref, f32[8,256,256]{2,1,0:T(8,128)S(1)} %get-tuple-element.8.fresh, f32[8,128]{1,0:T(8,128)S(1)} %get-tuple-element.9.mode_ref), custom_call_target="tpu_custom_call" | custom-call | tf_op jit(solution)/shard_map/solve/pallas_call | solution.py:590

commit v7 on v5

--- a/solution.py
+++ b/solution.py
@@ -277,16 +277,18 @@
             sums_ref[peer] = message
             build(peer, message)
 
+    paired = count - 1 - (count - 1) % 2
+
     def take_two(number, carry):
-        take((count - 1 - 2 * number, count - 2 - 2 * number))
+        take((paired - 2 * number, paired - 1 - 2 * number))
         return carry
 
     message = mine[...]
     sums_ref[own] = message
     build(own, message)
+    if (count - 1) % 2:
+        take((count - 1,))
     lax.fori_loop(0, (count - 1) // 2, take_two, 0)
-    if (count - 1) % 2:
-        take((1,))
     for copy in copies:
         copy.wait_send()
 

time: 14.3 us -> 14.4 us (level)
  no operation moved by 1% of the time
where the time goes in v7:
time: 14.4 us; the launch traced here: 14.2 us
  Pallas kernels  12.9 us (90%)
  between operations  1.28 us (9%)
    pallas_call x1, Pallas kernels, local(): pl.pallas_call(functools.partial(share_kernel, 'tm'), out_shape=(jax.Shap...  9.68 us
    pallas_call x1, Pallas kernels, local(): pl.pallas_call(functools.partial(solve_kernel, 'tm', 'rows'), out_shape=(...  3.22 us

profile of v7, /device:TPU:0, one launch (start us, length us, event | category | flops | bytes accessed | tf_op | source)
XLA Modules:
  0.0 14.2 jit_solution(14578579248036190974)
XLA Ops:
  1.3 9.7 %share.1 = (f32[8,16,128]{2,1,0:T(8,128)S(1)}, f32[8,8,128]{2,1,0:T(8,128)S(1)}, f32[8,256,256]{2,1,0:T(8,128)S(1)}, f32[8,128]{1,0:T(8,128)S(1)}) custom-call(s32[1]{0:T(128)S(6)} %copy.8.counts_ref, s32[16,128]{1,0:T(8,128)} %bitcast.5, f32[16,128]{1,0:T(8,128)} %bitcast.6, f32[1,128]{1,0:T(1,128)} %bitcast.7, f32[1,128]{1,0:T(1,128)} %bitcast.8, ...), custom_call_target="tpu_custom_call" | custom-call | tf_op jit(solution)/shard_map/share/pallas_call | solution.py:559
  11.0 3.2 %solve.1 = (f32[1,64]{1,0:T(1,128)}, f32[1,64,256]{2,1,0:T(8,128)}) custom-call(f32[8,16,128]{2,1,0:T(8,128)S(1)} %get-tuple-element.6.sums_ref, f32[8,8,128]{2,1,0:T(8,128)S(1)} %get-tuple-element.7.turn_ref, f32[8,256,256]{2,1,0:T(8,128)S(1)} %get-tuple-element.8.fresh, f32[8,128]{1,0:T(8,128)S(1)} %get-tuple-element.9.mode_ref), custom_call_target="tpu_custom_call" | custom-call | tf_op jit(solution)/shard_map/solve/pallas_call | solution.py:592
